TPU v7x, 768 devices: a whole 4x8x12 slice. The times are simulated.
768 devices in a mesh: fsdp: 48 (over z, y_lo), seq: 16 (over y_hi, x, core).
Axes of the slice: x: 4, y: 8 (y_hi: 2, y_lo: 4; y = y_hi * 4 + y_lo), z: 12, core: 2. Of those that a mesh axis runs over, the one named last changes fastest.
Arguments:
- tokens: bfloat16 [48, 2048, 2304], P('fsdp', 'seq'), may hold values from -6 to 6
- queries: bfloat16 [48, 2048, 2048], P('fsdp', 'seq'), may hold values from -9 to 9
- key_rows: bfloat16 [48, 2048, 512], P('fsdp', 'seq'), may hold values from -9 to 9
- out_grad: bfloat16 [48, 2048, 2048], P('fsdp', 'seq'), may hold values from -0.0625 to 0.0625
- value_weight: bfloat16 [2304, 512], P('fsdp'), may hold values from -0.125 to 0.125
- documents: int32 [48, 2048], P('fsdp'), may hold values from 0 to 15, never falling along the last dimension, each value on 1 to 512 neighbouring positions
- block_plan: int32 [48, 16], P('fsdp'), may hold values from 0 to 15, each once within a row
Outputs:
- attended: bfloat16 [48, 2048, 2048], P('fsdp', 'seq')
- weight_grad: float32 [2304, 512], P(('fsdp', 'seq'))
Inputs may be any that keep to these rules, and one draw needn't show every extreme that they name: `documents`: document numbers never fall along a sequence; each document covers at most 512 places, and one covers exactly that many. `block_plan`: each row names every block of its sequence once.
All inputs are finite; a program needn't handle non-finite values.
Results may differ from a plain program's by a relative error of at most 0.018.
Values may be sent and summed in bfloat16 or wider, within the bound.
A program may use at most 32 MiB of HBM per device.

v0:
```python
import jax
import jax.numpy as jnp
from jax import lax
from jax.sharding import PartitionSpec as P

QH = 16
KH = 4
HD = 128
BLOCK = 128


def split_blocks(array, block_rows):
    return array.reshape((array.shape[0] // block_rows, block_rows) + array.shape[1:])


def block_weights(query_block, place_block, segment_block, key_set, positions, segment_ids):
    scores = jnp.einsum(
        "qhd,khd->hqk", query_block, key_set, preferred_element_type=jnp.float32
    ) * HD ** (-0.5)
    visible = (segment_block[:, None] == segment_ids[None, :]) & (
        positions[None, :] <= place_block[:, None]
    )
    scores = jnp.where(visible[None], scores, -jnp.inf)
    row_max = jnp.max(scores, axis=2, keepdims=True)
    exponent = jnp.exp(scores - row_max)
    return (exponent / jnp.sum(exponent, axis=2, keepdims=True)).astype(jnp.bfloat16)


def attend_forward(received, positions, segment_ids):
    query_set, key_set, value_set = received
    block_rows = min(512, query_set.shape[0])
    blocks = (
        split_blocks(query_set, block_rows),
        split_blocks(positions, block_rows),
        split_blocks(segment_ids, block_rows),
    )

    def attend_block(running, inputs):
        weights = block_weights(inputs[0], inputs[1], inputs[2], key_set, positions, segment_ids)
        outputs = jnp.einsum(
            "hqk,khd->qhd", weights, value_set, preferred_element_type=jnp.float32
        ).astype(jnp.bfloat16)
        return (running, (outputs, weights))

    unused, stacked = lax.scan(attend_block, jnp.zeros((), jnp.float32), blocks)
    return (stacked[0].reshape(query_set.shape), stacked[1])


def partial_rows(columns, grad_rows):
    product = lax.dot_general(
        columns, grad_rows, (((0,), (0,)), ((), ())), preferred_element_type=jnp.float32
    )
    rounded = lax.optimization_barrier(product.astype(jnp.bfloat16))
    return rounded.astype(jnp.float32)


def shards(tokens, queries, key_rows, out_grad, value_weight, documents, block_plan):
    features = tokens[0]
    tok_rows = features.shape[0]
    values = jnp.dot(
        features,
        lax.all_gather(value_weight, "fsdp", axis=0, tiled=True),
        preferred_element_type=jnp.float32,
    ).astype(jnp.bfloat16)
    group_size = QH // KH
    query_heads = queries[0].reshape(tok_rows, QH, HD)
    key_heads = jnp.repeat(key_rows[0].reshape(tok_rows, KH, HD), group_size, axis=1)
    value_heads = jnp.repeat(values.reshape(tok_rows, KH, HD), group_size, axis=1)
    grad_heads = out_grad[0].reshape(tok_rows, QH, HD)
    block_count = block_plan.shape[1]
    offsets = jnp.arange(BLOCK, dtype=jnp.int32)
    positions = (block_plan[0][:, None] * BLOCK + offsets[None, :]).reshape(block_count * BLOCK)
    segment_ids = (
        documents[0].reshape(block_count, BLOCK)[block_plan[0]].reshape(block_count * BLOCK)
    )
    lane_count = lax.axis_size("seq")
    received = (
        lax.all_to_all(query_heads, "seq", split_axis=1, concat_axis=0, tiled=True),
        lax.all_to_all(key_heads, "seq", split_axis=1, concat_axis=0, tiled=True),
        lax.all_to_all(value_heads, "seq", split_axis=1, concat_axis=0, tiled=True),
    )
    outputs, weights = attend_forward(received, positions, segment_ids)
    back_out = lax.all_to_all(outputs, "seq", split_axis=0, concat_axis=1, tiled=True)
    grad_set = lax.all_to_all(grad_heads, "seq", split_axis=1, concat_axis=0, tiled=True)
    block_rows = weights.shape[2]
    head_grads = jnp.einsum(
        "chqk,cqhd->khd",
        weights,
        split_blocks(grad_set, block_rows),
        preferred_element_type=jnp.float32,
    ).astype(jnp.bfloat16)
    back_grad = lax.all_to_all(head_grads, "seq", split_axis=0, concat_axis=1, tiled=True)
    attended = back_out.reshape(1, tok_rows, QH * HD)
    value_grad = jnp.sum(
        back_grad.reshape(tok_rows, KH, group_size, HD).astype(jnp.float32), axis=2
    )
    value_grad = value_grad.astype(jnp.bfloat16).reshape(tok_rows, KH * HD)
    owner_count = lax.axis_size("fsdp")
    feature_count = features.shape[1]
    owned_rows = feature_count // (owner_count * lane_count)
    ordered = features.reshape(tok_rows, owner_count, lane_count, owned_rows).transpose(0, 2, 1, 3)
    ordered = ordered.reshape(tok_rows, feature_count)
    lane_sums = lax.psum_scatter(
        partial_rows(ordered, value_grad).astype(jnp.bfloat16),
        "seq",
        scatter_dimension=0,
        tiled=True,
    ).astype(jnp.float32)
    weight_grad = lax.psum_scatter(lane_sums, "fsdp", scatter_dimension=0, tiled=True)
    return (attended, weight_grad)


def solution(mesh):
    in_specs = (
        P("fsdp", "seq", None),
        P("fsdp", "seq", None),
        P("fsdp", "seq", None),
        P("fsdp", "seq", None),
        P("fsdp", None),
        P("fsdp", None),
        P("fsdp", None),
    )
    out_specs = (P("fsdp", "seq", None), P(("fsdp", "seq"), None))
    return jax.shard_map(shards, mesh=mesh, in_specs=in_specs, out_specs=out_specs, check_vma=False)
```

profile of v0, /device:TPU:6, one launch (start us, length us, event | category | flops | bytes accessed | tf_op | source)
XLA Modules:
  0.0 678.0 jit_solution(2640076051667188029)
XLA Ops:
  7.9 2.0 copy.48
  10.0 13.0 %all-to-all-start = ((bf16[128,16,128]{0,2,1:T(8,128)(2,1)}), bf16[128,16,128]{0,2,1:T(8,128)(2,1)S(1)}, u32[]{:S(2)}, u32[]{:S(2)}) async-start(bf16[128,16,128]{0,2,1:T(8,128)(2,1)} %bitcast.4), calls=%async_computation | async-start | bytes 1048576 | tf_op jit(solution)/shard_map/all_to_all | solution.py:78
  23.9 12.9 %all-to-all-done = bf16[128,16,128]{0,2,1:T(8,128)(2,1)S(1)} async-done(((bf16[128,16,128]{0,2,1:T(8,128)(2,1)}), bf16[128,16,128]{0,2,1:T(8,128)(2,1)S(1)}, u32[]{:S(2)}, u32[]{:S(2)}) %all-to-all-start) | async-done | bytes 524320 | tf_op jit(solution)/shard_map/all_to_all | solution.py:78
  37.7 9.8 %all-to-all-start.1 = ((bf16[128,16,128]{2,0,1:T(8,128)(2,1)}), bf16[128,16,128]{2,0,1:T(8,128)(2,1)S(1)}, u32[]{:S(2)}, u32[]{:S(2)}) async-start(bf16[128,16,128]{2,0,1:T(8,128)(2,1)} %bitcast.9), calls=%async_computation.1 | async-start | bytes 1048576 | tf_op jit(solution)/shard_map/all_to_all | solution.py:79
  47.5 201.0 %all-gather.2.cloned.1.call-done = bf16[2304,512]{1,0:T(8,128)(2,1)} async-done(((bf16[48,512]{1,0:T(8,128)(2,1)}), bf16[2304,512]{1,0:T(8,128)(2,1)}) %all-gather.2.cloned.1.call-update) | async-done | bytes 2359312 | tf_op jit(solution)/shard_map/all_gather | solution.py:62
  248.5 2.1 fusion.22
  251.6 8.5 %all-to-all-start.2 = ((bf16[128,16,128]{2,0,1:T(8,128)(2,1)}), bf16[128,16,128]{2,0,1:T(8,128)(2,1)S(1)}, u32[]{:S(2)}, u32[]{:S(2)}) async-start(bf16[128,16,128]{2,0,1:T(8,128)(2,1)} %bitcast.14), calls=%async_computation.2 | async-start | bytes 1048576 | tf_op jit(solution)/shard_map/all_to_all | solution.py:80
  260.9 1.0 copy.55
  262.3 11.6 %all-to-all-done.2 = bf16[128,16,128]{2,0,1:T(8,128)(2,1)S(1)} async-done(((bf16[128,16,128]{2,0,1:T(8,128)(2,1)}), bf16[128,16,128]{2,0,1:T(8,128)(2,1)S(1)}, u32[]{:S(2)}, u32[]{:S(2)}) %all-to-all-start.2) | async-done | bytes 524320 | tf_op jit(solution)/shard_map/all_to_all | solution.py:80
  273.9 8.9 %all-to-all-start.4 = ((bf16[128,16,128]{2,0,1:T(8,128)(2,1)}), bf16[128,16,128]{2,0,1:T(8,128)(2,1)S(1)}, u32[]{:S(2)}, u32[]{:S(2)}) async-start(bf16[128,16,128]{2,0,1:T(8,128)(2,1)} %copy.55), calls=%async_computation.4 | async-start | bytes 1048576 | tf_op jit(solution)/shard_map/all_to_all | solution.py:84
  282.8 19.3 %while.13 = (s32[]{:T(128)}, bf16[4,512,1,128]{3,1,2,0:T(8,128)(2,1)S(1)}, bf16[4,1,512,2048]{3,2,1,0:T(8,128)(2,1)}, s32[4,512]{1,0:T(4,128)S(1)}, s32[16,128]{...) while((s32[]{:T(128)}, ...), condition=%wide.region_3.4_spmd.clone, body=%wide.region_0.3_spmd.clone.sunk | while | flops 548471808 | bytes 20232888 | solution.py:45
  282.9 1.1 fusion.38
  284.7 2.1 bitcast_dynamic-update-slice_fusion.2
  287.7 1.1 fusion.38
  289.6 2.1 bitcast_dynamic-update-slice_fusion.2
  292.5 1.1 fusion.38
  294.4 2.1 bitcast_dynamic-update-slice_fusion.2
  297.3 1.1 fusion.38
  299.2 2.1 bitcast_dynamic-update-slice_fusion.2
  302.1 6.0 fusion.19
  308.6 1.0 reduce.10
  310.6 9.6 %all-to-all-start.5 = ((bf16[16,2,8192]{2,1,0:T(2,128)(2,1)}), bf16[16,2,8192]{2,1,0:T(2,128)(2,1)S(1)}, u32[]{:S(2)}, u32[]{:S(2)}) async-start(bf16[16,2,8192]{2,1,0:T(2,128)(2,1)} %reshape.162), calls=%async_computation.5 | async-start | bytes 1048576 | tf_op jit(solution)/shard_map/all_to_all | solution.py:92
  321.8 10.9 %all-to-all-done.5 = bf16[16,2,8192]{2,1,0:T(2,128)(2,1)S(1)} async-done(((bf16[16,2,8192]{2,1,0:T(2,128)(2,1)}), bf16[16,2,8192]{2,1,0:T(2,128)(2,1)S(1)}, u32[]{:S(2)}, u32[]{:S(2)}) %all-to-all-start.5) | async-done | bytes 524320 | tf_op jit(solution)/shard_map/all_to_all | solution.py:92
  334.3 2.5 copy.64
  336.9 1.0 reduce.9
  338.8 7.1 %all-to-all-start.3 = ((bf16[16,2,8192]{2,1,0:T(2,128)(2,1)}), bf16[16,2,8192]{2,1,0:T(2,128)(2,1)S(1)}, u32[]{:S(2)}, u32[]{:S(2)}) async-start(bf16[16,2,8192]{2,1,0:T(2,128)(2,1)} %reshape.164), calls=%async_computation.3 | async-start | bytes 1048576 | tf_op jit(solution)/shard_map/all_to_all | solution.py:83
  345.9 1.3 dynamic-slice
  347.8 10.6 %all-to-all-done.3 = bf16[16,2,8192]{2,1,0:T(2,128)(2,1)S(1)} async-done(((bf16[16,2,8192]{2,1,0:T(2,128)(2,1)}), bf16[16,2,8192]{2,1,0:T(2,128)(2,1)S(1)}, u32[]{:S(2)}, u32[]{:S(2)}) %all-to-all-start.3) | async-done | bytes 524320 | tf_op jit(solution)/shard_map/all_to_all | solution.py:83
  359.3 1.0 copy.61
  360.4 78.1 %reduce-scatter.5.cloned.1.call-done = bf16[144,512]{1,0:T(8,128)(2,1)} async-done(((bf16[2304,512]{1,0:T(8,128)(2,1)}), bf16[144,512]{1,0:T(8,128)(2,1)}) %reduce-scatter.5.cloned.1.call-update) | async-done | bytes 147472
  438.4 1.0 copy.65
  439.5 230.8 %all-reduce.2 = f32[144,512]{0,1:T(8,128)S(1)} all-reduce(bf16[144,512]{0,1:T(8,128)(2,1)S(1)} %copy.65), channel_id=3, replica_groups=mesh['fsdp'=48,'seq'=16] {'fsdp'}, use_global_device_ids=true, to_apply=%region_6.7.clone | all-reduce | flops 73728 | bytes 442368
  (69 shorter events, 18.2 us)
Async XLA Ops:
  7.2 253.1 %copy-start = (s32[1,2048]{1,0:T(1,128)S(1)}, s32[1,2048]{1,0:T(1,128)}, u32[]{:S(2)}) copy-start(s32[1,2048]{1,0:T(1,128)} %param.14) | copy-start | bytes 24580
  7.2 241.3 %copy-start.1 = (bf16[1,128,2304]{2,1,0:T(8,128)(2,1)S(1)}, bf16[1,128,2304]{2,1,0:T(8,128)(2,1)}, u32[]{:S(2)}) copy-start(bf16[1,128,2304]{2,1,0:T(8,128)(2,1)} %param.9) | copy-start | bytes 1769476
  7.2 241.3 %all-gather.2.cloned.1.call-start = ((), (), s32[]{:S(2)}) async-start(), calls=%async_computation.7 | async-start | bytes 2408448 | tf_op jit(solution)/shard_map/all_gather | solution.py:62
  10.0 250.1 %copy-start.5 = (s32[1,16]{1,0:T(1,128)S(1)}, s32[1,16]{1,0:T(1,128)}, u32[]{:S(2)}) copy-start(s32[1,16]{1,0:T(1,128)} %param.15) | copy-start | bytes 196
  10.0 250.8 %copy-start.2 = (bf16[1,128,2048]{2,1,0:T(8,128)(2,1)S(1)}, bf16[1,128,2048]{2,1,0:T(8,128)(2,1)}, u32[]{:S(2)}) copy-start(bf16[1,128,2048]{2,1,0:T(8,128)(2,1)} %param.12) | copy-start | bytes 1572868
  10.0 26.8 %all-to-all-start = ((bf16[128,16,128]{0,2,1:T(8,128)(2,1)}), bf16[128,16,128]{0,2,1:T(8,128)(2,1)S(1)}, u32[]{:S(2)}, u32[]{:S(2)}) async-start(bf16[128,16,128]{0,2,1:T(8,128)(2,1)} %bitcast.4), calls=%async_computation | async-start | bytes 1048576 | tf_op jit(solution)/shard_map/all_to_all | solution.py:78
  37.7 213.0 %all-to-all-start.1 = ((bf16[128,16,128]{2,0,1:T(8,128)(2,1)}), bf16[128,16,128]{2,0,1:T(8,128)(2,1)S(1)}, u32[]{:S(2)}, u32[]{:S(2)}) async-start(bf16[128,16,128]{2,0,1:T(8,128)(2,1)} %bitcast.9), calls=%async_computation.1 | async-start | bytes 1048576 | tf_op jit(solution)/shard_map/all_to_all | solution.py:79
  251.6 22.3 %all-to-all-start.2 = ((bf16[128,16,128]{2,0,1:T(8,128)(2,1)}), bf16[128,16,128]{2,0,1:T(8,128)(2,1)S(1)}, u32[]{:S(2)}, u32[]{:S(2)}) async-start(bf16[128,16,128]{2,0,1:T(8,128)(2,1)} %bitcast.14), calls=%async_computation.2 | async-start | bytes 1048576 | tf_op jit(solution)/shard_map/all_to_all | solution.py:80
  273.9 28.2 %all-to-all-start.4 = ((bf16[128,16,128]{2,0,1:T(8,128)(2,1)}), bf16[128,16,128]{2,0,1:T(8,128)(2,1)S(1)}, u32[]{:S(2)}, u32[]{:S(2)}) async-start(bf16[128,16,128]{2,0,1:T(8,128)(2,1)} %copy.55), calls=%async_computation.4 | async-start | bytes 1048576 | tf_op jit(solution)/shard_map/all_to_all | solution.py:84
  302.1 6.0 copy-start.3
  310.6 22.1 %all-to-all-start.5 = ((bf16[16,2,8192]{2,1,0:T(2,128)(2,1)}), bf16[16,2,8192]{2,1,0:T(2,128)(2,1)S(1)}, u32[]{:S(2)}, u32[]{:S(2)}) async-start(bf16[16,2,8192]{2,1,0:T(2,128)(2,1)} %reshape.162), calls=%async_computation.5 | async-start | bytes 1048576 | tf_op jit(solution)/shard_map/all_to_all | solution.py:92
  320.2 118.2 %reduce-scatter.5.cloned.1.call-start = ((), (), s32[]{:S(2)}) async-start(), calls=%async_computation.8 | async-start | bytes 2506752
  334.3 2.5 copy-start.4
  338.8 19.6 %all-to-all-start.3 = ((bf16[16,2,8192]{2,1,0:T(2,128)(2,1)}), bf16[16,2,8192]{2,1,0:T(2,128)(2,1)S(1)}, u32[]{:S(2)}, u32[]{:S(2)}) async-start(bf16[16,2,8192]{2,1,0:T(2,128)(2,1)} %reshape.164), calls=%async_computation.3 | async-start | bytes 1048576 | tf_op jit(solution)/shard_map/all_to_all | solution.py:83
Sparse Core Ops, SparseCore 0:
  10.4 238.0 all-gather.1
  337.0 101.4 reduce-scatter.4
where the time goes:
time: 679 us; the launch traced here: 678 us
  waiting for transfers between devices  326 us (48%)
  blocking collectives  231 us (34%)
  starting transfers between devices  57 us (8%)
  local copies, waits for them, and re-layouts  19.2 us (3%)
  matrix products  16.6 us (2%)
  between operations  15 us (2%)
  other arithmetic  13.7 us (2%)
    unnamed x1, blocking collectives  231 us
    all_gather x1, waiting for transfers between devices, shards(): lax.all_gather(value_weight, 'fsdp', axis=0, tiled=True)  201 us
    unnamed x3, waiting for transfers between devices  78.8 us
  transfers between devices with their start and end apart: 8, of which 6 were waited for; matrix products, arithmetic and copies ran while one was open for 5% of the time, Pallas kernels for 0%

commit v1 on v0

v1 whole, which is shorter than its diff:
```python
import jax
import jax.numpy as jnp
from jax import lax
from jax.experimental import pallas as pl
from jax.experimental.pallas import tpu as pltpu
from jax.sharding import PartitionSpec as P

BLOCK = 128
HD = 128
GROUP = 4
NX, NY, NZ, NYL = 4, 8, 12, 4
BF16 = jnp.bfloat16
F32 = jnp.float32
MESH = pl.DeviceIdType.MESH


def body(
    tok_hbm, q_hbm, k_hbm, do_hbm, w_hbm, docs_ref, plan_ref,
    att_out, wg_out,
    tok2, q2, do2, kall, vall, wbuf, bias, wts, slots, dvs, dvr, dvt, vgp, att2,
    gs, gr, ysum, xf, xs, xr, xsum, zs, zr, cs, cr,
    lsem, es, er, wys, wyr, wzs, wzr, ks, kr, vs, vr, ds_, dr, gys, gyr, xss, xrs, zss, zrs,
):
    f = lax.axis_index("fsdp")
    s = lax.axis_index("seq")
    z, yl = f // NYL, f % NYL
    yh, x, c = s // 8, (s // 2) % NX, s % 2
    y = yh * NYL + yl
    chip = s // 2

    def dev(z_, y_, x_, c_):
        return (z_ * NYL + y_ % NYL, (y_ // NYL) * 8 + x_ * 2 + c_)

    xp, xm, x2 = (x + 1) % NX, (x + 3) % NX, (x + 2) % NX
    core_dev = dev(z, y, x, 1 - c)
    xp_dev, xm_dev, x2_dev = dev(z, y, xp, c), dev(z, y, xm, c), dev(z, y, x2, c)
    yp_dev, ym_dev = dev(z, (y + 1) % NY, x, c), dev(z, (y + 7) % NY, x, c)
    yp2_dev, ym2_dev = dev(z, (y + 2) % NY, x, c), dev(z, (y + 6) % NY, x, c)
    y4_dev = dev(z, (y + 4) % NY, x, c)
    zp_dev, zm_dev = dev((z + 1) % NZ, y, x, c), dev((z + 11) % NZ, y, x, c)

    barrier = pltpu.get_barrier_semaphore()
    near = [core_dev, xp_dev, xm_dev, x2_dev, yp_dev, ym_dev, yp2_dev, ym2_dev, y4_dev]
    for d in range(1, NZ):
        pl.semaphore_signal(barrier, inc=1, device_id=dev((z + d) % NZ, y, x, c), device_id_type=MESH)
    for target in near:
        pl.semaphore_signal(barrier, inc=1, device_id=target, device_id_type=MESH)
    pl.semaphore_wait(barrier, len(near) + NZ - 1)

    def remote(src, dst, ssem, rsem, target):
        return pltpu.make_async_remote_copy(
            src_ref=src, dst_ref=dst, send_sem=ssem, recv_sem=rsem,
            device_id=target, device_id_type=MESH,
        )

    started = []

    def send(src, dst, ssem, rsem, target):
        copy = remote(src, dst, ssem, rsem, target)
        copy.start()
        started.append(copy)
        return copy

    col = pl.ds(pl.multiple_of(c * 256, 256), 256)
    other_col = pl.ds(pl.multiple_of((1 - c) * 256, 256), 256)
    wide = pl.ds(pl.multiple_of(c * 1024, 1024), 1024)
    other_wide = pl.ds(pl.multiple_of((1 - c) * 1024, 1024), 1024)

    ek = send(k_hbm.at[:, other_col], kall.at[s], es.at[0], er.at[0], core_dev)
    lk = pltpu.make_async_copy(k_hbm.at[:, col], kall.at[s], lsem.at[0])
    lk.start()
    w_own = w_hbm.at[:, col]
    wy = [
        None,
        send(w_own, wbuf.at[f], wys.at[1], wyr.at[1], ym_dev),
        send(w_own, wbuf.at[f], wys.at[2], wyr.at[2], yp2_dev),
        send(w_own, wbuf.at[f], wys.at[3], wyr.at[3], yp_dev),
    ]
    lw = pltpu.make_async_copy(w_own, wbuf.at[f], lsem.at[1])
    lw.start()

    def ring_copies(t, i):
        cls = (yl + i) % NYL
        plus = ((z + NZ - (t - 1)) % NZ) * NYL + cls
        out = [remote(wbuf.at[plus], wbuf.at[plus], wzs.at[0, t - 1, i], wzr.at[0, t - 1, i], zp_dev)]
        minus = ((z + t - 1) % NZ) * NYL + cls
        out.append(remote(wbuf.at[minus], wbuf.at[minus], wzs.at[1, t - 1, i], wzr.at[1, t - 1, i], zm_dev))
        return out

    z_first = [
        send(w_own, wbuf.at[f], wzs.at[0, 0, 0], wzr.at[0, 0, 0], zp_dev),
        send(w_own, wbuf.at[f], wzs.at[1, 0, 0], wzr.at[1, 0, 0], zm_dev),
    ]
    eq = send(q_hbm.at[:, other_wide], q2.at[c], es.at[1], er.at[1], core_dev)
    lq = pltpu.make_async_copy(q_hbm.at[:, wide], q2.at[c], lsem.at[2])
    lq.start()
    ed = send(do_hbm.at[:, other_wide], do2.at[c], es.at[2], er.at[2], core_dev)
    ld = pltpu.make_async_copy(do_hbm.at[:, wide], do2.at[c], lsem.at[3])
    ld.start()
    et = send(tok_hbm, tok2.at[c], es.at[3], er.at[3], core_dev)
    lt = pltpu.make_async_copy(tok_hbm, tok2.at[c], lsem.at[4])
    lt.start()

    def gather_start(buf, ss, rs):
        own = buf.at[pl.ds(2 * chip, 2)]
        return [
            send(own, own, ss.at[0], rs.at[0], y4_dev),
            send(own, own, ss.at[1], rs.at[1], xp_dev),
            send(own, own, ss.at[2], rs.at[2], xm_dev),
        ]

    def gather_own_forward(buf, ss, rs, first):
        first[1].wait_recv()
        a = buf.at[2 * (yh * NX + xm)]
        up = send(a, a, ss.at[5], rs.at[5], xp_dev)
        first[2].wait_recv()
        b = buf.at[2 * (yh * NX + xp) + 1]
        down = send(b, b, ss.at[6], rs.at[6], xm_dev)
        return [up, down]

    def gather_peer(buf, ss, rs, first):
        first[0].wait_recv()
        peer = buf.at[pl.ds(2 * ((1 - yh) * NX + x), 2)]
        return [
            send(peer, peer, ss.at[3], rs.at[3], xp_dev),
            send(peer, peer, ss.at[4], rs.at[4], xm_dev),
        ]

    def gather_peer_forward(buf, ss, rs, second):
        second[0].wait_recv()
        a = buf.at[2 * ((1 - yh) * NX + xm)]
        up = send(a, a, ss.at[7], rs.at[7], xp_dev)
        second[1].wait_recv()
        b = buf.at[2 * ((1 - yh) * NX + xp) + 1]
        down = send(b, b, ss.at[8], rs.at[8], xm_dev)
        return [up, down]

    lk.wait()
    ek.wait_recv()
    k_first = gather_start(kall, ks, kr)
    for i in (1, 3, 2):
        wy[i].wait_recv()
        for copy in ring_copies(1, i):
            copy.start()
            started.append(copy)

    def ring_step(t):
        for i in (0, 1, 3, 2):
            before = ring_copies(t - 1, i)
            after = ring_copies(t, i)
            before[0].wait_recv()
            after[0].start()
            started.append(after[0])
            before[1].wait_recv()
            if t <= 5:
                after[1].start()
                started.append(after[1])

    k_own = gather_own_forward(kall, ks, kr, k_first)
    ring_step(2)

    places = [plan_ref[0, 2 * chip + b] for b in range(2)]
    key_at = []
    row_i = lax.broadcasted_iota(jnp.int32, (BLOCK, BLOCK), 0)
    col_i = lax.broadcasted_iota(jnp.int32, (BLOCK, BLOCK), 1)
    for b in range(2):
        rows = docs_ref[pl.ds(places[b], 1), :].astype(F32)
        ats = []
        for j in range(5):
            place = places[b] - j
            at = jnp.int32(0)
            for t in range(16):
                at = jnp.where(plan_ref[0, t] == place, t, at)
            ats.append(at)
            keys = docs_ref[pl.ds(jnp.maximum(place, 0), 1), :].astype(F32)
            keys = jnp.where(place >= 0, keys, jnp.float32(-1.0))
            keys = jnp.broadcast_to(keys, (BLOCK, BLOCK))
            column = jnp.sum(jnp.where(row_i == col_i, keys, 0.0), axis=1, keepdims=True)
            seen = jnp.broadcast_to(column, (BLOCK, BLOCK)) == jnp.broadcast_to(rows, (BLOCK, BLOCK))
            if j == 0:
                seen = seen & (row_i <= col_i)
            bias[b, pl.ds(j * BLOCK, BLOCK), :] = jnp.where(seen, jnp.float32(0.0), jnp.float32(-jnp.inf))
        key_at.append(ats)

    k_second = gather_peer(kall, ks, kr, k_first)
    ring_step(3)
    k_third = gather_peer_forward(kall, ks, kr, k_second)
    lq.wait()
    eq.wait_recv()
    ld.wait()
    ed.wait_recv()
    ring_step(4)
    for copy in k_own + k_third:
        copy.wait_recv()

    def weigh(b):
        def group(g, carry):
            lanes = pl.ds(pl.multiple_of(g * HD, HD), HD)
            keys = jnp.concatenate([kall[at, :, lanes] for at in key_at[b]], axis=0)
            total = jnp.zeros((5 * BLOCK, HD), F32)
            for h in range(GROUP):
                head = pl.ds(pl.multiple_of((g * GROUP + h) * HD, HD), HD)
                scores = lax.dot_general(
                    keys, q2[b, :, head], (((1,), (1,)), ((), ())), preferred_element_type=F32
                ) * F32(HD ** -0.5) + bias[b]
                peak = jnp.max(scores, axis=0, keepdims=True)
                exponent = jnp.exp(scores - peak)
                inverse = 1.0 / jnp.sum(exponent, axis=0, keepdims=True)
                weights = (exponent * inverse).astype(BF16)
                wts[b, g * GROUP + h] = weights
                total = total + jnp.dot(weights, do2[b, :, head], preferred_element_type=F32)
            for j in range(5):
                slots[b, j, :, lanes] = total[j * BLOCK:(j + 1) * BLOCK]
            return carry

        lax.fori_loop(0, 2, group, 0)
        slots[b, 5] = jnp.zeros((BLOCK, 256), F32)

    weigh(0)
    ring_step(5)
    weigh(1)

    def lay(t, carry):
        place = plan_ref[0, t]
        parts = []
        for b in range(2):
            j = places[b] - place
            j = jnp.where((j >= 0) & (j <= 4), j, 5)
            parts.append(slots[b, j])
        dvs[t // 8, (t // 2) % NX, t % 2] = (parts[0] + parts[1]).astype(BF16)
        return carry

    lax.fori_loop(0, 16, lay, 0)

    da = send(dvs.at[:, x2, 0], dvr.at[0], ds_.at[0], dr.at[0], xp_dev)
    db = send(dvs.at[:, x2, 1], dvr.at[1], ds_.at[1], dr.at[1], xm_dev)
    dc = send(dvs.at[:, xp, 1], dvr.at[2], ds_.at[2], dr.at[2], xp_dev)
    dd = send(dvs.at[:, xm, 0], dvr.at[3], ds_.at[3], dr.at[3], xm_dev)

    ring_step(6)
    lt.wait()
    et.wait_recv()
    lw.wait()
    for i in range(NYL):
        ring_copies(6, i)[0].wait_recv()
    weight = wbuf[...].reshape(48 * 48, 256)
    for b in range(2):
        vall[2 * chip + b] = jnp.dot(tok2[b], weight, preferred_element_type=F32).astype(BF16)

    def add_pair(dst, a, b):
        dst[...] = (a[...].astype(F32) + b[...].astype(F32)).astype(BF16)

    da.wait_recv()
    for k in range(2):
        dvt[0, k] = (dvs[k, xp, 0].astype(F32) + dvr[0, k].astype(F32)).astype(BF16)
    de = send(dvt.at[0], dvr.at[4], ds_.at[4], dr.at[4], xp_dev)
    db.wait_recv()
    for k in range(2):
        dvt[1, k] = (dvs[k, xm, 1].astype(F32) + dvr[1, k].astype(F32)).astype(BF16)
    df = send(dvt.at[1], dvr.at[5], ds_.at[5], dr.at[5], xm_dev)
    v_first = gather_start(vall, vs, vr)
    dc.wait_recv()
    dd.wait_recv()
    de.wait_recv()
    df.wait_recv()

    def chip_total(k, b):
        one, two = (3, 4) if b == 0 else (2, 5)
        return dvs[k, x, b].astype(F32) + dvr[one, k].astype(F32) + dvr[two, k].astype(F32)

    for b in range(2):
        vgp[0, b] = chip_total(1 - yh, b).astype(BF16)
    dy = send(vgp.at[0], vgp.at[1], ds_.at[6], dr.at[6], y4_dev)
    v_own = gather_own_forward(vall, vs, vr, v_first)
    dy.wait_recv()
    value_grad = [
        (chip_total(yh, b) + vgp[1, b].astype(F32)).astype(BF16) for b in range(2)
    ]

    for j in range(6):
        lanes = pl.ds(j * 384, 384)
        product = jnp.zeros((384, 256), F32)
        for b in range(2):
            product = product + lax.dot_general(
                tok2[b, :, lanes], value_grad[b], (((0,), (0,)), ((), ())), preferred_element_type=F32
            )
        for a in range(NYL):
            for h in range(2):
                at = (a * 2 + h) * 24
                pair = jnp.concatenate([product[at:at + 24], product[192 + at:192 + at + 24]], axis=0)
                gs[h * NYL + a, pl.ds(j * 48, 48), :] = pair.astype(BF16)

    halves = (pl.ds(0, 144), pl.ds(144, 144))
    streams = ((0, 0, 4), (1, 1, 4), (0, 1, 3), (1, 0, 3))
    y_dev = (yp_dev, ym_dev)

    def y_dest(direction, distance):
        return (y + distance) % NY if direction == 0 else (y + NY - distance) % NY

    def y_copy(stream, hop):
        direction, half, hops = streams[stream]
        at = y_dest(direction, hops - hop)
        return remote(
            gs.at[at, halves[half]], gr.at[stream, hop], gys.at[stream, hop], gyr.at[stream, hop], y_dev[direction]
        )

    flying = []
    for stream in range(4):
        copy = y_copy(stream, 0)
        copy.start()
        started.append(copy)
        flying.append(copy)
    for hop in range(1, 4):
        for stream in range(4):
            direction, half, hops = streams[stream]
            if hop >= hops:
                continue
            flying[stream].wait_recv()
            at = y_dest(direction, hops - hop)
            gs[at, halves[half], :] = (
                gs[at, halves[half], :].astype(F32) + gr[stream, hop - 1].astype(F32)
            ).astype(BF16)
            copy = y_copy(stream, hop)
            copy.start()
            started.append(copy)
            flying[stream] = copy
    v_second = gather_peer(vall, vs, vr, v_first)
    v_third = gather_peer_forward(vall, vs, vr, v_second)
    for stream in range(4):
        flying[stream].wait_recv()
    for half in range(2):
        ysum[halves[half], :] = (
            gs[y, halves[half], :].astype(F32)
            + gr[0 if half == 0 else 2, 3 if half == 0 else 2].astype(F32)
            + gr[3 if half == 0 else 1, 2 if half == 0 else 3].astype(F32)
        )

    for k in range(NX):
        for j in range(NZ):
            xf[k, pl.ds(j * 6, 6), :] = ysum[pl.ds(j * 24 + k * 6, 6), :]
    for k in range(NX):
        xs[k] = xf[k].astype(BF16)
    x_copies = [
        send(xs.at[xp], xr.at[0], xss.at[0], xrs.at[0], xp_dev),
        send(xs.at[xm], xr.at[1], xss.at[1], xrs.at[1], xm_dev),
        send(xs.at[x2], xr.at[2], xss.at[2], xrs.at[2], x2_dev),
    ]

    for copy in v_own + v_third:
        copy.wait_recv()

    def attend(b):
        def group(g, carry):
            lanes = pl.ds(pl.multiple_of(g * HD, HD), HD)
            held = jnp.concatenate([vall[at, :, lanes] for at in key_at[b]], axis=0)
            for h in range(GROUP):
                head = pl.ds(pl.multiple_of((g * GROUP + h) * HD, HD), HD)
                flipped = lax.dot_general(
                    held, wts[b, g * GROUP + h], (((0,), (0,)), ((), ())), preferred_element_type=F32
                )
                att2[b, :, head] = flipped.T.astype(BF16)
            return carry

        lax.fori_loop(0, 2, group, 0)

    for copy in x_copies:
        copy.wait_recv()
    xsum[...] = xf[x] + xr[0].astype(F32) + xr[1].astype(F32) + xr[2].astype(F32)

    zs[...] = jnp.zeros((NZ, 8, 256), F32)
    for j in range(NZ):
        zs[j, 0:6, :] = xsum[pl.ds(j * 6, 6), :]

    z_copies = []
    for d in range(1, NZ):
        there = (z + d) % NZ
        z_copies.append(send(zs.at[there], zr.at[d], zss.at[d], zrs.at[d], dev(there, y, x, c)))
    attend(0)
    attend(1)
    la = pltpu.make_async_copy(att2.at[c], att_out.at[:, wide], lsem.at[5])
    la.start()
    ea = send(att2.at[1 - c], att_out.at[:, wide], es.at[4], er.at[4], core_dev)
    total = zs[z]
    for d in range(1, NZ):
        z_copies[d - 1].wait_recv()
        total = total + zr[d]
    cs[...] = jnp.zeros((2, 8, 256), F32)
    cs[0, 0:3, :] = total[0:3]
    cs[1, 0:3, :] = total[3:6]
    ec = send(cs.at[1 - c], cr, es.at[5], er.at[5], core_dev)
    ec.wait_recv()
    mine, theirs = cs[c], cr[...]
    wg_out[:, 0:256] = jnp.where(c == 0, mine, theirs)[0:3]
    wg_out[:, 256:512] = jnp.where(c == 0, theirs, mine)[0:3]
    la.wait()
    ea.wait_recv()
    for copy in started:
        copy.wait_send()


def shards(tokens, queries, key_rows, out_grad, value_weight, documents, block_plan):
    anywhere = pl.BlockSpec(memory_space=pl.ANY)
    in_vmem = pl.BlockSpec(memory_space=pltpu.VMEM)
    dma = pltpu.SemaphoreType.DMA
    vmem = pltpu.VMEM
    attended, weight_grad = pl.pallas_call(
        body,
        out_shape=(
            jax.ShapeDtypeStruct((BLOCK, 2048), BF16),
            jax.ShapeDtypeStruct((3, 512), F32),
        ),
        in_specs=[anywhere] * 5 + [in_vmem, pl.BlockSpec(memory_space=pltpu.SMEM)],
        out_specs=(anywhere, in_vmem),
        scratch_shapes=[
            vmem((2, BLOCK, 2304), BF16),
            vmem((2, BLOCK, 1024), BF16),
            vmem((2, BLOCK, 1024), BF16),
            vmem((16, BLOCK, 256), BF16),
            vmem((16, BLOCK, 256), BF16),
            vmem((48, 48, 256), BF16),
            vmem((2, 5 * BLOCK, BLOCK), F32),
            vmem((2, 8, 5 * BLOCK, BLOCK), BF16),
            vmem((2, 6, BLOCK, 256), F32),
            vmem((2, NX, 2, BLOCK, 256), BF16),
            vmem((6, 2, BLOCK, 256), BF16),
            vmem((2, 2, BLOCK, 256), BF16),
            vmem((2, 2, BLOCK, 256), BF16),
            vmem((2, BLOCK, 1024), BF16),
            vmem((NY, 288, 256), BF16),
            vmem((4, 4, 144, 256), BF16),
            vmem((288, 256), F32),
            vmem((NX, 72, 256), F32),
            vmem((NX, 72, 256), BF16),
            vmem((3, 72, 256), BF16),
            vmem((72, 256), F32),
            vmem((NZ, 8, 256), F32),
            vmem((NZ, 8, 256), F32),
            vmem((2, 8, 256), F32),
            vmem((8, 256), F32),
            dma((6,)),
            dma((6,)), dma((6,)),
            dma((4,)), dma((4,)),
            dma((2, 6, 4)), dma((2, 6, 4)),
            dma((9,)), dma((9,)),
            dma((9,)), dma((9,)),
            dma((7,)), dma((7,)),
            dma((4, 4)), dma((4, 4)),
            dma((3,)), dma((3,)),
            dma((NZ,)), dma((NZ,)),
        ],
        compiler_params=pltpu.CompilerParams(
            collective_id=0, has_side_effects=True, vmem_limit_bytes=60 * 1024 * 1024
        ),
        name="value_path",
    )(
        tokens[0], queries[0], key_rows[0], out_grad[0], value_weight,
        documents.reshape(16, BLOCK), block_plan,
    )
    return attended[None], weight_grad


def solution(mesh):
    in_specs = (
        P("fsdp", "seq", None),
        P("fsdp", "seq", None),
        P("fsdp", "seq", None),
        P("fsdp", "seq", None),
        P("fsdp", None),
        P("fsdp", None),
        P("fsdp", None),
    )
    out_specs = (P("fsdp", "seq", None), P(("fsdp", "seq"), None))
    return jax.shard_map(shards, mesh=mesh, in_specs=in_specs, out_specs=out_specs, check_vma=False)
```

time: 679 us -> 100 us (0.15)
  the two profiles are of different devices: /device:TPU:6 before, /device:TPU:1 now
where the time goes in v1:
time: 100 us
  Pallas kernels  96.9 us (97%)
  local copies, waits for them, and re-layouts  2.49 us (2%)
    pallas_call x1, Pallas kernels, shards(): pl.pallas_call(body, out_shape=(jax.ShapeDtypeStruct((BLOCK, 2048), BF16)...  96.9 us
    unnamed x4, local copies, waits for them, and re-layouts  2.49 us

profile of v1, /device:TPU:1, one launch (start us, length us, event | category | flops | bytes accessed | tf_op | source)
XLA Modules:
  0.0 100.1 jit_solution(18407228174375780171)
XLA Ops:
  0.6 96.9 %value_path.1 = (bf16[128,2048]{1,0:T(8,128)(2,1)}, f32[3,512]{1,0:T(4,128)}) custom-call(bf16[128,2304]{1,0:T(8,128)(2,1)} %bitcast.6, bf16[128,2048]{1,0:T(8,128)(2,1)} %bitcast.8, bf16[128,512]{1,0:T(8,128)(2,1)} %bitcast.10, bf16[128,2048]{1,0:T(8,128)(2,1)} %bitcast.9, bf16[48,512]{1,0:T(8,128)(2,1)} %w_hbm.1, s32[16,128]{1,0:T(8,128)} %bitcast.11, ...), custom_call_target="tpu_custom_call" | custom-call | tf_op jit(solution)/shard_map/value_path/pallas_call | solution.py:406
  97.6 0.0 copy-start
  97.6 1.9 %copy.11 = bf16[1,128,2048]{2,1,0:T(8,128)(2,1)} copy(bf16[1,128,2048]{2,1,0:T(8,128)(2,1)} %bitcast.7) | data formatting | bytes 1048576
  99.5 0.0 copy-done
  99.5 0.6 copy.12
Async XLA Ops:
  97.6 1.9 %copy-start = (f32[3,512]{1,0:T(4,128)S(1)}, f32[3,512]{1,0:T(4,128)}, u32[]{:S(2)}) copy-start(f32[3,512]{1,0:T(4,128)} %get-tuple-element.9) | copy-start | bytes 18436

commit v2 on v1

v2 whole, which is shorter than its diff:
```python
import jax
import jax.numpy as jnp
from jax import lax
from jax.experimental import pallas as pl
from jax.experimental.pallas import tpu as pltpu
from jax.sharding import PartitionSpec as P

BLOCK = 128
HD = 128
GROUP = 4
NX, NY, NZ, NYL = 4, 8, 12, 4
LOG2E = 1.4426950408889634
BF16 = jnp.bfloat16
F32 = jnp.float32
MESH = pl.DeviceIdType.MESH


def body(
    tok_hbm, q_hbm, k_hbm, do_hbm, w_hbm, docs_ref, plan_ref,
    att_out, wg_out,
    tok2, q2, do2, kall, vall, wbuf, bias, wts, slots, dvs, dvr, dvt, vgp, att2,
    gs, gr, ysum, xf, xs, xr, xsum, gb, xb, xbs, xbr, xbt, yb, ybs, ybr, bsum, zs, zr,
    lsem, es, er, wys, wyr, wzs, wzr, ks, kr, vs, vr, ds_, dr, dys, dyr, gys, gyr, xss, xrs, bs, br, bys, byr, zss, zrs,
):
    f = lax.axis_index("fsdp")
    s = lax.axis_index("seq")
    z, yl = f // NYL, f % NYL
    yh, x, c = s // 8, (s // 2) % NX, s % 2
    y = yh * NYL + yl
    chip = s // 2

    def dev(z_, y_, x_, c_):
        return (z_ * NYL + y_ % NYL, (y_ // NYL) * 8 + x_ * 2 + c_)

    xp, xm, x2 = (x + 1) % NX, (x + 3) % NX, (x + 2) % NX
    core_dev = dev(z, y, x, 1 - c)
    xp_dev, xm_dev, x2_dev = dev(z, y, xp, c), dev(z, y, xm, c), dev(z, y, x2, c)
    yp_dev, ym_dev = dev(z, (y + 1) % NY, x, c), dev(z, (y + 7) % NY, x, c)
    yp2_dev, ym2_dev = dev(z, (y + 2) % NY, x, c), dev(z, (y + 6) % NY, x, c)
    yp3_dev, ym3_dev = dev(z, (y + 3) % NY, x, c), dev(z, (y + 5) % NY, x, c)
    y4_dev = dev(z, (y + 4) % NY, x, c)
    zp_dev, zm_dev = dev((z + 1) % NZ, y, x, c), dev((z + 11) % NZ, y, x, c)

    barrier = pltpu.get_barrier_semaphore()
    near = [
        y4_dev, yp3_dev, ym3_dev, yp2_dev, ym2_dev, x2_dev, xp_dev, xm_dev, yp_dev, ym_dev, zp_dev, zm_dev, core_dev,
    ]
    for target in near:
        pl.semaphore_signal(barrier, inc=1, device_id=target, device_id_type=MESH)
    pl.semaphore_wait(barrier, len(near))

    def remote(src, dst, ssem, rsem, target):
        return pltpu.make_async_remote_copy(
            src_ref=src, dst_ref=dst, send_sem=ssem, recv_sem=rsem,
            device_id=target, device_id_type=MESH,
        )

    started = []

    def send(src, dst, ssem, rsem, target):
        copy = remote(src, dst, ssem, rsem, target)
        copy.start()
        started.append(copy)
        return copy

    col = pl.ds(pl.multiple_of(c * 256, 256), 256)
    other_col = pl.ds(pl.multiple_of((1 - c) * 256, 256), 256)
    wide = pl.ds(pl.multiple_of(c * 1024, 1024), 1024)
    other_wide = pl.ds(pl.multiple_of((1 - c) * 1024, 1024), 1024)

    ek = send(k_hbm.at[:, other_col], kall.at[s], es.at[0], er.at[0], core_dev)
    lk = pltpu.make_async_copy(k_hbm.at[:, col], kall.at[s], lsem.at[0])
    lk.start()
    w_own = w_hbm.at[:, col]
    send(w_own, wbuf.at[f], wzs.at[0, 0, 0], wzr.at[0, 0, 0], zp_dev)
    send(w_own, wbuf.at[f], wzs.at[1, 0, 0], wzr.at[1, 0, 0], zm_dev)
    wy = [
        None,
        send(w_own, wbuf.at[f], wys.at[1], wyr.at[1], ym_dev),
        send(w_own, wbuf.at[f], wys.at[2], wyr.at[2], yp2_dev),
        send(w_own, wbuf.at[f], wys.at[3], wyr.at[3], yp_dev),
    ]
    lw = pltpu.make_async_copy(w_own, wbuf.at[f], lsem.at[1])
    lw.start()
    eq = send(q_hbm.at[:, other_wide], q2.at[c], es.at[1], er.at[1], core_dev)
    lq = pltpu.make_async_copy(q_hbm.at[:, wide], q2.at[c], lsem.at[2])
    lq.start()
    ed = send(do_hbm.at[:, other_wide], do2.at[c], es.at[2], er.at[2], core_dev)
    ld = pltpu.make_async_copy(do_hbm.at[:, wide], do2.at[c], lsem.at[3])
    ld.start()
    et = send(tok_hbm, tok2.at[c], es.at[3], er.at[3], core_dev)
    lt = pltpu.make_async_copy(tok_hbm, tok2.at[c], lsem.at[4])
    lt.start()

    def unit(row, column, block):
        return 2 * (row * NX + column) + block

    def gather_y(buf, ss, rs):
        out = []
        for block, sem in ((0, 0), (1, 9)):
            own = buf.at[unit(yh, x, block)]
            out.append(send(own, own, ss.at[sem], rs.at[sem], y4_dev))
        return out

    def gather_x(buf, ss, rs):
        out = []
        for block, sem, target in ((0, 1, xp_dev), (1, 2, xm_dev), (1, 12, xp_dev), (0, 13, xm_dev)):
            own = buf.at[unit(yh, x, block)]
            out.append(send(own, own, ss.at[sem], rs.at[sem], target))
        return out

    def gather_x_forward(buf, ss, rs, first):
        first[0].wait_recv()
        a = buf.at[unit(yh, xm, 0)]
        up = send(a, a, ss.at[5], rs.at[5], xp_dev)
        first[1].wait_recv()
        b = buf.at[unit(yh, xp, 1)]
        down = send(b, b, ss.at[6], rs.at[6], xm_dev)
        return [first[2], first[3], up, down]

    def gather_peer(buf, ss, rs, from_y, block):
        from_y[block].wait_recv()
        peer = buf.at[unit(1 - yh, x, block)]
        sems = (3, 4) if block == 0 else (10, 11)
        out = [
            send(peer, peer, ss.at[sems[0]], rs.at[sems[0]], xp_dev),
            send(peer, peer, ss.at[sems[1]], rs.at[sems[1]], xm_dev),
        ]
        return out

    def gather_peer_forward(buf, ss, rs, peer, block):
        if block == 0:
            peer[0].wait_recv()
            a = buf.at[unit(1 - yh, xm, 0)]
            return [peer[1], send(a, a, ss.at[7], rs.at[7], xp_dev)]
        peer[1].wait_recv()
        b = buf.at[unit(1 - yh, xp, 1)]
        return [peer[0], send(b, b, ss.at[8], rs.at[8], xm_dev)]

    def ring_plus(t, i):
        at = ((z + NZ - (t - 1)) % NZ) * NYL + (yl + i) % NYL
        return remote(wbuf.at[at], wbuf.at[at], wzs.at[0, t - 1, i], wzr.at[0, t - 1, i], zp_dev)

    def ring_minus(t, i):
        at = ((z + t - 1) % NZ) * NYL + (yl + i) % NYL
        return remote(wbuf.at[at], wbuf.at[at], wzs.at[1, t - 1, i], wzr.at[1, t - 1, i], zm_dev)

    def ring_step(t):
        for i in (0, 1, 3, 2):
            ring_plus(t - 1, i).wait_recv()
            copy = ring_plus(t, i)
            copy.start()
            started.append(copy)
            ring_minus(t - 1, i).wait_recv()
            if t <= 5:
                copy = ring_minus(t, i)
                copy.start()
                started.append(copy)

    lk.wait()
    ek.wait_recv()
    k_y = gather_y(kall, ks, kr)
    k_x = gather_x(kall, ks, kr)

    places = [plan_ref[0, 2 * chip + b] for b in range(2)]
    key_at = []
    row_i = lax.broadcasted_iota(jnp.int32, (BLOCK, BLOCK), 0)
    col_i = lax.broadcasted_iota(jnp.int32, (BLOCK, BLOCK), 1)
    for b in range(2):
        rows = docs_ref[pl.ds(places[b], 1), :].astype(F32)
        ats = []
        for j in range(5):
            place = places[b] - j
            at = jnp.int32(0)
            for t in range(16):
                at = jnp.where(plan_ref[0, t] == place, t, at)
            ats.append(at)
            keys = docs_ref[pl.ds(jnp.maximum(place, 0), 1), :].astype(F32)
            keys = jnp.where(place >= 0, keys, jnp.float32(-1.0))
            keys = jnp.broadcast_to(keys, (BLOCK, BLOCK))
            column = jnp.sum(jnp.where(row_i == col_i, keys, 0.0), axis=1, keepdims=True)
            seen = jnp.broadcast_to(column, (BLOCK, BLOCK)) == jnp.broadcast_to(rows, (BLOCK, BLOCK))
            if j == 0:
                seen = seen & (row_i <= col_i)
            bias[b, pl.ds(j * BLOCK, BLOCK), :] = jnp.where(seen, jnp.float32(0.0), jnp.float32(-jnp.inf))
        key_at.append(ats)
    for i in (1, 3, 2):
        wy[i].wait_recv()
        for copy in (ring_plus(1, i), ring_minus(1, i)):
            copy.start()
            started.append(copy)
    k_rest = gather_x_forward(kall, ks, kr, k_x)
    k_peer0 = gather_peer(kall, ks, kr, k_y, 0)
    ring_step(2)
    k_peer1 = gather_peer(kall, ks, kr, k_y, 1)
    k_rest += gather_peer_forward(kall, ks, kr, k_peer0, 0)
    ring_step(3)
    k_rest += gather_peer_forward(kall, ks, kr, k_peer1, 1)
    lq.wait()
    eq.wait_recv()
    ld.wait()
    ed.wait_recv()
    ring_step(4)
    for copy in k_rest:
        copy.wait_recv()

    def weigh(b):
        def group(g):
            lanes = pl.ds(g * HD, HD)
            keys = jnp.concatenate([kall[at, :, lanes] for at in key_at[b]], axis=0)
            total = jnp.zeros((5 * BLOCK, HD), F32)
            for h in range(GROUP):
                head = pl.ds(pl.multiple_of((g * GROUP + h) * HD, HD), HD)
                scores = lax.dot_general(
                    keys, q2[b, :, head], (((1,), (1,)), ((), ())), preferred_element_type=F32
                ) + bias[b]
                peak = jnp.max(scores, axis=0, keepdims=True)
                exponent = jnp.exp2((scores - peak) * F32(HD ** -0.5 * LOG2E))
                inverse = 1.0 / jnp.sum(exponent, axis=0, keepdims=True)
                weights = (exponent * inverse).astype(BF16)
                wts[b, g * GROUP + h] = weights
                total = total + jnp.dot(weights, do2[b, :, head], preferred_element_type=F32)
            for j in range(5):
                slots[b, j, :, lanes] = total[j * BLOCK:(j + 1) * BLOCK]

        return group

    weigh(0)(0)
    ring_step(5)
    weigh(0)(1)
    weigh(1)(0)
    ring_step(6)
    weigh(1)(1)
    for b in range(2):
        slots[b, 5] = jnp.zeros((BLOCK, 256), F32)

    def lay(t, carry):
        place = plan_ref[0, t]
        parts = []
        for b in range(2):
            j = places[b] - place
            j = jnp.where((j >= 0) & (j <= 4), j, 5)
            parts.append(slots[b, j])
        dvs[t // 8, (t // 2) % NX, t % 2] = (parts[0] + parts[1]).astype(BF16)
        return carry

    lax.fori_loop(0, 16, lay, 0)

    sides = (1 - yh, yh)

    def dv_send(src, number, side, target):
        return send(src, dvr.at[number, side], ds_.at[number, side], dr.at[number, side], target)

    far, close, joint = [], [], []
    for side in range(2):
        far.append((
            dv_send(dvs.at[sides[side], x2, 0], 0, side, xp_dev),
            dv_send(dvs.at[sides[side], x2, 1], 1, side, xm_dev),
        ))
        if side == 0:
            close.append((
                dv_send(dvs.at[sides[side], xp, 1], 2, side, xp_dev),
                dv_send(dvs.at[sides[side], xm, 0], 3, side, xm_dev),
            ))
    lt.wait()
    et.wait_recv()
    lw.wait()
    for i in range(NYL):
        ring_plus(6, i).wait_recv()
    weight = wbuf[...].reshape(48 * 48, 256)
    for b in range(2):
        vall[2 * chip + b] = jnp.dot(tok2[b], weight, preferred_element_type=F32).astype(BF16)
    v_y = gather_y(vall, vs, vr)

    for side in range(2):
        ends = []
        for way in range(2):
            far[side][way].wait_recv()
            mine = dvs[sides[side], xp, 0] if way == 0 else dvs[sides[side], xm, 1]
            dvt[way, side] = (mine.astype(F32) + dvr[way, side].astype(F32)).astype(BF16)
            ends.append(dv_send(dvt.at[way, side], 4 + way, side, xp_dev if way == 0 else xm_dev))
        joint.append(ends)
        if side == 0:
            close.append((
                dv_send(dvs.at[sides[1], xp, 1], 2, 1, xp_dev),
                dv_send(dvs.at[sides[1], xm, 0], 3, 1, xm_dev),
            ))

    def chip_total(side, b):
        for copy in (close[side][1 - b], joint[side][b]):
            copy.wait_recv()
        one, two = (3, 4) if b == 0 else (2, 5)
        return dvs[sides[side], x, b].astype(F32) + dvr[one, side].astype(F32) + dvr[two, side].astype(F32)

    to_y = []
    for b in range(2):
        vgp[0, b] = chip_total(0, b).astype(BF16)
        to_y.append(send(vgp.at[0, b], vgp.at[1, b], dys.at[b], dyr.at[b], y4_dev))
    v_x = gather_x(vall, vs, vr)
    held_total = [chip_total(1, b) for b in range(2)]
    v_rest = gather_x_forward(vall, vs, vr, v_x)
    value_grad = []
    for b in range(2):
        to_y[b].wait_recv()
        value_grad.append((held_total[b] + vgp[1, b].astype(F32)).astype(BF16))

    for j in range(6):
        lanes = pl.ds(j * 384, 384)
        product = jnp.zeros((384, 256), F32)
        for b in range(2):
            product = product + lax.dot_general(
                tok2[b, :, lanes], value_grad[b], (((0,), (0,)), ((), ())), preferred_element_type=F32
            )
        for a in range(NYL):
            for h in range(2):
                at = (a * 2 + h) * 24
                pair = jnp.concatenate(
                    [product[at:at + 24, 0:HD], product[192 + at:192 + at + 24, 0:HD]], axis=0
                )
                gs[h * NYL + a, pl.ds(j * 48, 48), :] = pair.astype(BF16)
        gb[pl.ds(j * 384, 384), :] = product[:, HD:2 * HD]

    halves = (pl.ds(0, 144), pl.ds(144, 144))
    streams = ((0, 0, 4), (1, 1, 4), (0, 1, 3), (1, 0, 3))
    y_dev = (yp_dev, ym_dev)

    def y_dest(direction, distance):
        return (y + distance) % NY if direction == 0 else (y + NY - distance) % NY

    def y_send(stream, hop):
        direction, half, hops = streams[stream]
        at = y_dest(direction, hops - hop)
        return send(
            gs.at[at, halves[half]], gr.at[stream, hop], gys.at[stream, hop], gyr.at[stream, hop], y_dev[direction]
        )

    def y_hop(hop):
        for stream in range(4):
            direction, half, hops = streams[stream]
            if hop >= hops:
                continue
            flying[stream].wait_recv()
            at = y_dest(direction, hops - hop)
            gs[at, halves[half], :] = (
                gs[at, halves[half], :].astype(F32) + gr[stream, hop - 1].astype(F32)
            ).astype(BF16)
            flying[stream] = y_send(stream, hop)

    flying = [y_send(stream, 0) for stream in range(4)]

    for j in range(NZ):
        for a in range(NYL):
            for h in range(2):
                for k in range(NX):
                    to = (h * NYL + a) * 72 + j * 6
                    xb[k, pl.ds(to, 6), :] = gb[pl.ds(j * 192 + (a * 2 + h) * 24 + k * 6, 6), :]
    for k in range(NX):
        xbs[k] = xb[k].astype(BF16)
    sides_b = (pl.ds(0, 288), pl.ds(288, 288))

    def b_send(src, number, target):
        return send(src, xbr.at[number], bs.at[number], br.at[number], target)

    b_far = [
        b_send(xbs.at[x2, sides_b[0]], 0, xp_dev),
        b_send(xbs.at[x2, sides_b[1]], 1, xm_dev),
    ]
    b_close = [
        b_send(xbs.at[xp, sides_b[1]], 2, xp_dev),
        b_send(xbs.at[xm, sides_b[0]], 3, xm_dev),
    ]
    b_far[0].wait_recv()
    xbt[0] = (xb[xp, sides_b[0], :] + xbr[0].astype(F32)).astype(BF16)
    b_joint = [b_send(xbt.at[0], 4, xp_dev)]
    b_far[1].wait_recv()
    xbt[1] = (xb[xm, sides_b[1], :] + xbr[1].astype(F32)).astype(BF16)
    b_joint.append(b_send(xbt.at[1], 5, xm_dev))
    y_hop(1)
    for copy in (b_close[1], b_joint[0]):
        copy.wait_recv()
    yb[sides_b[0], :] = xb[x, sides_b[0], :] + xbr[3].astype(F32) + xbr[4].astype(F32)
    for copy in (b_close[0], b_joint[1]):
        copy.wait_recv()
    yb[sides_b[1], :] = xb[x, sides_b[1], :] + xbr[2].astype(F32) + xbr[5].astype(F32)
    for k in range(NY):
        ybs[k] = yb[pl.ds(k * 72, 72), :].astype(BF16)
    b_y = []
    for d in (4, 3, 5, 2, 6, 1, 7):
        there = (y + d) % NY
        b_y.append(send(ybs.at[there], ybr.at[d], bys.at[d], byr.at[d], dev(z, there, x, c)))
    y_hop(2)
    v_peer0 = gather_peer(vall, vs, vr, v_y, 0)
    v_peer1 = gather_peer(vall, vs, vr, v_y, 1)
    y_hop(3)
    for stream in range(4):
        flying[stream].wait_recv()
    for half in range(2):
        ysum[halves[half], :] = (
            gs[y, halves[half], :].astype(F32)
            + gr[0 if half == 0 else 2, 3 if half == 0 else 2].astype(F32)
            + gr[3 if half == 0 else 1, 2 if half == 0 else 3].astype(F32)
        )

    for k in range(NX):
        for j in range(NZ):
            xf[k, pl.ds(j * 6, 6), :] = ysum[pl.ds(j * 24 + k * 6, 6), :]
    for k in range(NX):
        xs[k] = xf[k].astype(BF16)
    x_copies = [
        send(xs.at[x2], xr.at[2], xss.at[2], xrs.at[2], x2_dev),
        send(xs.at[xp], xr.at[0], xss.at[0], xrs.at[0], xp_dev),
        send(xs.at[xm], xr.at[1], xss.at[1], xrs.at[1], xm_dev),
    ]
    v_rest += gather_peer_forward(vall, vs, vr, v_peer0, 0)
    v_rest += gather_peer_forward(vall, vs, vr, v_peer1, 1)
    for copy in b_y:
        copy.wait_recv()
    b_total = yb[pl.ds(pl.multiple_of(y * 72, 8), 72), :]
    for d in range(1, NY):
        b_total = b_total + ybr[d].astype(F32)
    bsum[...] = b_total
    for copy in x_copies:
        copy.wait_recv()
    xsum[...] = xf[x] + xr[0].astype(F32) + xr[1].astype(F32) + xr[2].astype(F32)

    zs[...] = jnp.zeros((NZ, 2, 8, HD), F32)
    for j in range(NZ):
        for core in range(2):
            at = pl.ds(j * 6 + core * 3, 3)
            zs[j, core, 0:3, :] = xsum[at, :]
            zs[j, core, 3:6, :] = bsum[at, :]

    z_copies = []
    for d in (6, 5, 7, 4, 8, 3, 9, 2, 10, 1, 11, 0):
        there = (z + d) % NZ
        if d > 0:
            z_copies.append(
                send(zs.at[there, c], zr.at[0, d], zss.at[0, d], zrs.at[0, d], dev(there, y, x, c))
            )
        z_copies.append(
            send(zs.at[there, 1 - c], zr.at[1, d], zss.at[1, d], zrs.at[1, d], dev(there, y, x, 1 - c))
        )

    for copy in v_rest:
        copy.wait_recv()

    def attend(b):
        def group(g, carry):
            lanes = pl.ds(pl.multiple_of(g * HD, HD), HD)
            held = jnp.concatenate([vall[at, :, lanes] for at in key_at[b]], axis=0)
            for h in range(GROUP):
                head = pl.ds(pl.multiple_of((g * GROUP + h) * HD, HD), HD)
                flipped = lax.dot_general(
                    held, wts[b, g * GROUP + h], (((0,), (0,)), ((), ())), preferred_element_type=F32
                )
                att2[b, :, head] = flipped.T.astype(BF16)
            return carry

        lax.fori_loop(0, 2, group, 0)

    attend(0)
    attend(1)
    la = pltpu.make_async_copy(att2.at[c], att_out.at[:, wide], lsem.at[5])
    la.start()
    ea = send(att2.at[1 - c], att_out.at[:, wide], es.at[4], er.at[4], core_dev)
    for copy in z_copies:
        copy.wait_recv()
    mine, theirs = zs[z, c], zr[1, 0]
    for d in range(1, NZ):
        mine = mine + zr[0, d]
        theirs = theirs + zr[1, d]
    low, high = jnp.where(c == 0, mine, theirs), jnp.where(c == 0, theirs, mine)
    wg_out[:, 0:128] = low[0:3]
    wg_out[:, 128:256] = low[3:6]
    wg_out[:, 256:384] = high[0:3]
    wg_out[:, 384:512] = high[3:6]
    la.wait()
    ea.wait_recv()
    for copy in started:
        copy.wait_send()


def shards(tokens, queries, key_rows, out_grad, value_weight, documents, block_plan):
    anywhere = pl.BlockSpec(memory_space=pl.ANY)
    in_vmem = pl.BlockSpec(memory_space=pltpu.VMEM)
    dma = pltpu.SemaphoreType.DMA
    vmem = pltpu.VMEM
    attended, weight_grad = pl.pallas_call(
        body,
        out_shape=(
            jax.ShapeDtypeStruct((BLOCK, 2048), BF16),
            jax.ShapeDtypeStruct((3, 512), F32),
        ),
        in_specs=[anywhere] * 5 + [in_vmem, pl.BlockSpec(memory_space=pltpu.SMEM)],
        out_specs=(anywhere, in_vmem),
        scratch_shapes=[
            vmem((2, BLOCK, 2304), BF16),
            vmem((2, BLOCK, 1024), BF16),
            vmem((2, BLOCK, 1024), BF16),
            vmem((16, BLOCK, 256), BF16),
            vmem((16, BLOCK, 256), BF16),
            vmem((48, 48, 256), BF16),
            vmem((2, 5 * BLOCK, BLOCK), F32),
            vmem((2, 8, 5 * BLOCK, BLOCK), BF16),
            vmem((2, 6, BLOCK, 256), F32),
            vmem((2, NX, 2, BLOCK, 256), BF16),
            vmem((6, 2, BLOCK, 256), BF16),
            vmem((2, 2, BLOCK, 256), BF16),
            vmem((2, 2, BLOCK, 256), BF16),
            vmem((2, BLOCK, 1024), BF16),
            vmem((NY, 288, HD), BF16),
            vmem((4, 4, 144, HD), BF16),
            vmem((288, HD), F32),
            vmem((NX, 72, HD), F32),
            vmem((NX, 72, HD), BF16),
            vmem((3, 72, HD), BF16),
            vmem((72, HD), F32),
            vmem((2304, HD), F32),
            vmem((NX, 576, HD), F32),
            vmem((NX, 576, HD), BF16),
            vmem((6, 288, HD), BF16),
            vmem((2, 288, HD), BF16),
            vmem((576, HD), F32),
            vmem((NY, 72, HD), BF16),
            vmem((NY, 72, HD), BF16),
            vmem((72, HD), F32),
            vmem((NZ, 2, 8, HD), F32),
            vmem((2, NZ, 8, HD), F32),
            dma((6,)),
            dma((5,)), dma((5,)),
            dma((4,)), dma((4,)),
            dma((2, 6, 4)), dma((2, 6, 4)),
            dma((14,)), dma((14,)),
            dma((14,)), dma((14,)),
            dma((6, 2)), dma((6, 2)),
            dma((2,)), dma((2,)),
            dma((4, 4)), dma((4, 4)),
            dma((3,)), dma((3,)),
            dma((6,)), dma((6,)),
            dma((NY,)), dma((NY,)),
            dma((2, NZ)), dma((2, NZ)),
        ],
        compiler_params=pltpu.CompilerParams(
            collective_id=0, has_side_effects=True, vmem_limit_bytes=60 * 1024 * 1024
        ),
        name="value_path",
    )(
        tokens[0], queries[0], key_rows[0], out_grad[0], value_weight,
        documents.reshape(16, BLOCK), block_plan,
    )
    return attended[None], weight_grad


def solution(mesh):
    in_specs = (
        P("fsdp", "seq", None),
        P("fsdp", "seq", None),
        P("fsdp", "seq", None),
        P("fsdp", "seq", None),
        P("fsdp", None),
        P("fsdp", None),
        P("fsdp", None),
    )
    out_specs = (P("fsdp", "seq", None), P(("fsdp", "seq"), None))
    return jax.shard_map(shards, mesh=mesh, in_specs=in_specs, out_specs=out_specs, check_vma=False)
```

time: 100 us -> 93.1 us (0.931)
  Pallas kernels: 96.9 us -> 89.8 us
    pallas_call x1, Pallas kernels: 96.9 us -> 89.8 us  [shards(): pl.pallas_call(body, out_shape=(jax.ShapeDtypeStruct((BLOCK, 2048), BF16)...]
where the time goes in v2:
time: 93.1 us; the launch traced here: 92.9 us
  Pallas kernels  89.8 us (96%)
  local copies, waits for them, and re-layouts  2.49 us (3%)
    pallas_call x1, Pallas kernels, shards(): pl.pallas_call(body, out_shape=(jax.ShapeDtypeStruct((BLOCK, 2048), BF16)...  89.8 us
    unnamed x4, local copies, waits for them, and re-layouts  2.49 us

profile of v2, /device:TPU:1, one launch (start us, length us, event | category | flops | bytes accessed | tf_op | source)
XLA Modules:
  0.0 92.9 jit_solution(10096274682421176485)
XLA Ops:
  0.6 89.8 %value_path.1 = (bf16[128,2048]{1,0:T(8,128)(2,1)}, f32[3,512]{1,0:T(4,128)}) custom-call(bf16[128,2304]{1,0:T(8,128)(2,1)} %bitcast.6, bf16[128,2048]{1,0:T(8,128)(2,1)} %bitcast.8, bf16[128,512]{1,0:T(8,128)(2,1)} %bitcast.10, bf16[128,2048]{1,0:T(8,128)(2,1)} %bitcast.9, bf16[48,512]{1,0:T(8,128)(2,1)} %w_hbm.1, s32[16,128]{1,0:T(8,128)} %bitcast.11, ...), custom_call_target="tpu_custom_call" | custom-call | tf_op jit(solution)/shard_map/value_path/pallas_call | solution.py:488
  90.4 0.0 copy-start
  90.4 1.9 %copy.11 = bf16[1,128,2048]{2,1,0:T(8,128)(2,1)} copy(bf16[1,128,2048]{2,1,0:T(8,128)(2,1)} %bitcast.7) | data formatting | bytes 1048576
  92.3 0.0 copy-done
  92.3 0.6 copy.12
Async XLA Ops:
  90.4 1.9 %copy-start = (f32[3,512]{1,0:T(4,128)S(1)}, f32[3,512]{1,0:T(4,128)}, u32[]{:S(2)}) copy-start(f32[3,512]{1,0:T(4,128)} %get-tuple-element.9) | copy-start | bytes 18436

commit v3 on v2

v3 whole, which is shorter than its diff:
```python
import jax
import jax.numpy as jnp
from jax import lax
from jax.experimental import pallas as pl
from jax.experimental.pallas import tpu as pltpu
from jax.sharding import PartitionSpec as P

BLOCK = 128
HD = 128
GROUP = 4
NX, NY, NZ, NYL = 4, 8, 12, 4
LOG2E = 1.4426950408889634
BF16 = jnp.bfloat16
F32 = jnp.float32
MESH = pl.DeviceIdType.MESH


def body(
    tok_hbm, q_hbm, k_hbm, do_hbm, w_hbm, docs_ref, plan_ref,
    att_out, wg_out,
    tok2, q2, do2, kall0, kall1, vall, wbuf, bias, wts, slots, dvs, dvr, dvt, vgp, att2,
    gb, xb, xbs, xbr, xbt, yb, ybs, ybr, bsum, zs, zr,
    lsem, es, er, wys, wyr, wzs, wzr, ks, kr, vs, vr, ds_, dr, dys, dyr, bs, br, bys, byr, zss, zrs,
):
    f = lax.axis_index("fsdp")
    s = lax.axis_index("seq")
    z, yl = f // NYL, f % NYL
    yh, x, c = s // 8, (s // 2) % NX, s % 2
    y = yh * NYL + yl
    chip = s // 2

    def dev(z_, y_, x_, c_):
        return (z_ * NYL + y_ % NYL, (y_ // NYL) * 8 + x_ * 2 + c_)

    xp, xm, x2 = (x + 1) % NX, (x + 3) % NX, (x + 2) % NX
    core_dev = dev(z, y, x, 1 - c)
    xp_dev, xm_dev, x2_dev = dev(z, y, xp, c), dev(z, y, xm, c), dev(z, y, x2, c)
    yp_dev, ym_dev = dev(z, (y + 1) % NY, x, c), dev(z, (y + 7) % NY, x, c)
    yp2_dev, ym2_dev = dev(z, (y + 2) % NY, x, c), dev(z, (y + 6) % NY, x, c)
    yp3_dev, ym3_dev = dev(z, (y + 3) % NY, x, c), dev(z, (y + 5) % NY, x, c)
    y4_dev = dev(z, (y + 4) % NY, x, c)
    crossed = [dev(z, (y + 4) % NY, x, 1 - c), dev(z, y, xp, 1 - c), dev(z, y, xm, 1 - c)]
    zp_dev, zm_dev = dev((z + 1) % NZ, y, x, c), dev((z + 11) % NZ, y, x, c)

    barrier = pltpu.get_barrier_semaphore()
    near = [
        y4_dev, yp3_dev, ym3_dev, yp2_dev, ym2_dev, x2_dev, xp_dev, xm_dev, yp_dev, ym_dev, zp_dev, zm_dev, core_dev,
    ] + crossed
    for target in near:
        pl.semaphore_signal(barrier, inc=1, device_id=target, device_id_type=MESH)
    pl.semaphore_wait(barrier, len(near))

    def remote(src, dst, ssem, rsem, target):
        return pltpu.make_async_remote_copy(
            src_ref=src, dst_ref=dst, send_sem=ssem, recv_sem=rsem,
            device_id=target, device_id_type=MESH,
        )

    started = []

    def send(src, dst, ssem, rsem, target):
        copy = remote(src, dst, ssem, rsem, target)
        copy.start()
        started.append(copy)
        return copy

    col = pl.ds(pl.multiple_of(c * 256, 256), 256)
    other_col = pl.ds(pl.multiple_of((1 - c) * 256, 256), 256)
    wide = pl.ds(pl.multiple_of(c * 1024, 1024), 1024)
    other_wide = pl.ds(pl.multiple_of((1 - c) * 1024, 1024), 1024)

    w_own = w_hbm.at[:, col]
    send(w_own, wbuf.at[f], wzs.at[0, 0, 0], wzr.at[0, 0, 0], zp_dev)
    send(w_own, wbuf.at[f], wzs.at[1, 0, 0], wzr.at[1, 0, 0], zm_dev)
    wy = [
        None,
        send(w_own, wbuf.at[f], wys.at[1], wyr.at[1], ym_dev),
        send(w_own, wbuf.at[f], wys.at[2], wyr.at[2], yp2_dev),
        send(w_own, wbuf.at[f], wys.at[3], wyr.at[3], yp_dev),
    ]
    lw = pltpu.make_async_copy(w_own, wbuf.at[f], lsem.at[1])
    lw.start()
    first_x, last_x = jnp.where(c == 0, xp, xm), jnp.where(c == 0, xm, xp)
    kall = (kall0, kall1)
    key_local, key_core = [], []
    for g in range(2):
        k_own = k_hbm.at[:, pl.ds(pl.multiple_of(c * 256 + g * HD, HD), HD)]
        k_other = k_hbm.at[:, pl.ds(pl.multiple_of((1 - c) * 256 + g * HD, HD), HD)]

        def key_out(kind, targets):
            send(k_own, kall[g].at[s], ks.at[g, kind, 0], kr.at[g, kind, c], targets[0])
            send(k_other, kall[g].at[s], ks.at[g, kind, 1], kr.at[g, kind, c], targets[1])

        key_out(0, (y4_dev, crossed[0]))
        key_core.append(send(k_other, kall[g].at[s], es.at[5 + g], er.at[5 + g], core_dev))
        copy = pltpu.make_async_copy(k_own, kall[g].at[s], lsem.at[6 + g])
        copy.start()
        key_local.append(copy)
        key_out(1 + c, (dev(z, y, first_x, c), dev(z, y, first_x, 1 - c)))
        key_out(2 - c, (dev(z, y, last_x, c), dev(z, y, last_x, 1 - c)))

    def unit(row, column, block):
        return 2 * (row * NX + column) + block

    def arrived(buf, ss, rs, kind, block):
        return remote(buf.at[0], buf.at[0], ss.at[kind, block], rs.at[kind, block], core_dev)

    def gather_y(buf, ss, rs):
        for block in range(2):
            own = buf.at[unit(yh, x, block)]
            send(own, own, ss.at[0, block], rs.at[0, block], y4_dev)

    def gather_x(buf, ss, rs):
        for block, kind, target in ((0, 1, xp_dev), (1, 2, xm_dev), (1, 1, xp_dev), (0, 2, xm_dev)):
            own = buf.at[unit(yh, x, block)]
            send(own, own, ss.at[kind, block], rs.at[kind, block], target)

    def pass_on(buf, ss, rs, row, kinds, number):
        arrived(buf, ss, rs, kinds[0], 0).wait_recv()
        a = buf.at[unit(row, xm, 0)]
        send(a, a, ss.at[number, 0], rs.at[number, 0], xp_dev)
        arrived(buf, ss, rs, kinds[1], 1).wait_recv()
        b = buf.at[unit(row, xp, 1)]
        send(b, b, ss.at[number, 1], rs.at[number, 1], xm_dev)

    def gather_x_forward(buf, ss, rs):
        pass_on(buf, ss, rs, yh, (1, 2), 5)

    def gather_peer(buf, ss, rs, block):
        arrived(buf, ss, rs, 0, block).wait_recv()
        peer = buf.at[unit(1 - yh, x, block)]
        for kind, target in ((3, xp_dev), (4, xm_dev)) if block == 0 else ((4, xm_dev), (3, xp_dev)):
            send(peer, peer, ss.at[kind, block], rs.at[kind, block], target)

    def gather_peer_forward(buf, ss, rs):
        pass_on(buf, ss, rs, 1 - yh, (3, 4), 6)

    def gather_done(buf, ss, rs):
        for kind, block in ((1, 1), (2, 0), (5, 0), (5, 1), (3, 1), (4, 0), (6, 0), (6, 1)):
            arrived(buf, ss, rs, kind, block).wait_recv()

    def ring_plus(t, i):
        at = ((z + NZ - (t - 1)) % NZ) * NYL + (yl + i) % NYL
        return remote(wbuf.at[at], wbuf.at[at], wzs.at[0, t - 1, i], wzr.at[0, t - 1, i], zp_dev)

    def ring_minus(t, i):
        at = ((z + t - 1) % NZ) * NYL + (yl + i) % NYL
        return remote(wbuf.at[at], wbuf.at[at], wzs.at[1, t - 1, i], wzr.at[1, t - 1, i], zm_dev)

    def ring_step(t):
        for i in (0, 1, 3, 2):
            ring_plus(t - 1, i).wait_recv()
            copy = ring_plus(t, i)
            copy.start()
            started.append(copy)
            ring_minus(t - 1, i).wait_recv()
            if t <= 5:
                copy = ring_minus(t, i)
                copy.start()
                started.append(copy)

    places = [plan_ref[0, 2 * chip + b] for b in range(2)]
    key_at = []
    row_i = lax.broadcasted_iota(jnp.int32, (BLOCK, BLOCK), 0)
    col_i = lax.broadcasted_iota(jnp.int32, (BLOCK, BLOCK), 1)
    for b in range(2):
        rows = docs_ref[pl.ds(places[b], 1), :].astype(F32)
        ats = []
        for j in range(5):
            place = places[b] - j
            at = jnp.int32(0)
            for t in range(16):
                at = jnp.where(plan_ref[0, t] == place, t, at)
            ats.append(at)
            keys = docs_ref[pl.ds(jnp.maximum(place, 0), 1), :].astype(F32)
            keys = jnp.where(place >= 0, keys, jnp.float32(-1.0))
            keys = jnp.broadcast_to(keys, (BLOCK, BLOCK))
            column = jnp.sum(jnp.where(row_i == col_i, keys, 0.0), axis=1, keepdims=True)
            seen = jnp.broadcast_to(column, (BLOCK, BLOCK)) == jnp.broadcast_to(rows, (BLOCK, BLOCK))
            if j == 0:
                seen = seen & (row_i <= col_i)
            bias[b, pl.ds(j * BLOCK, BLOCK), :] = jnp.where(seen, jnp.float32(0.0), jnp.float32(-jnp.inf))
        key_at.append(ats)
    keys_of = [(kall[g], ks.at[g], kr.at[g]) for g in range(2)]
    gather_x_forward(*keys_of[0])
    for i in (1, 3, 2):
        wy[i].wait_recv()
        for copy in (ring_plus(1, i), ring_minus(1, i)):
            copy.start()
            started.append(copy)
    eq = send(q_hbm.at[:, other_wide], q2.at[c], es.at[1], er.at[1], core_dev)
    lq = pltpu.make_async_copy(q_hbm.at[:, wide], q2.at[c], lsem.at[2])
    lq.start()
    ed = send(do_hbm.at[:, other_wide], do2.at[c], es.at[2], er.at[2], core_dev)
    ld = pltpu.make_async_copy(do_hbm.at[:, wide], do2.at[c], lsem.at[3])
    ld.start()
    et = send(tok_hbm, tok2.at[c], es.at[3], er.at[3], core_dev)
    lt = pltpu.make_async_copy(tok_hbm, tok2.at[c], lsem.at[4])
    lt.start()

    gather_x_forward(*keys_of[1])
    gather_peer(*keys_of[0], 0)
    gather_peer(*keys_of[0], 1)
    ring_step(2)
    gather_peer_forward(*keys_of[0])
    gather_peer(*keys_of[1], 0)
    gather_peer(*keys_of[1], 1)
    lq.wait()
    eq.wait_recv()
    ld.wait()
    ed.wait_recv()
    key_local[0].wait()
    key_core[0].wait_recv()
    gather_done(*keys_of[0])
    ring_step(3)

    def weigh(b):
        def group(g):
            lanes = pl.ds(g * HD, HD)
            keys = jnp.concatenate([kall[g][at] for at in key_at[b]], axis=0)
            total = jnp.zeros((5 * BLOCK, HD), F32)
            for h in range(GROUP):
                head = pl.ds(pl.multiple_of((g * GROUP + h) * HD, HD), HD)
                scores = lax.dot_general(
                    keys, q2[b, :, head], (((1,), (1,)), ((), ())), preferred_element_type=F32
                ) + bias[b]
                peak = jnp.max(scores, axis=0, keepdims=True)
                exponent = jnp.exp2((scores - peak) * F32(HD ** -0.5 * LOG2E))
                inverse = 1.0 / jnp.sum(exponent, axis=0, keepdims=True)
                weights = (exponent * inverse).astype(BF16)
                wts[b, g * GROUP + h] = weights
                total = total + jnp.dot(weights, do2[b, :, head], preferred_element_type=F32)
            for j in range(5):
                slots[b, j, :, lanes] = total[j * BLOCK:(j + 1) * BLOCK]

        return group

    for b in range(2):
        slots[b, 5] = jnp.zeros((BLOCK, 256), F32)

    def lay(g):
        lanes = pl.ds(g * HD, HD)

        def one(t, carry):
            place = plan_ref[0, t]
            parts = []
            for b in range(2):
                j = places[b] - place
                j = jnp.where((j >= 0) & (j <= 4), j, 5)
                parts.append(slots[b, j, :, lanes])
            dvs[g, t // 8, (t // 2) % NX, t % 2] = (parts[0] + parts[1]).astype(BF16)
            return carry

        lax.fori_loop(0, 16, one, 0)

    sides = (1 - yh, yh)
    far, close, joint, to_y, held_total = {}, {}, {}, {}, {}

    def dv_send(g, src, number, side, target):
        return send(src, dvr.at[g, number, side], ds_.at[g, number, side], dr.at[g, number, side], target)

    def dv_out(g, side):
        row = sides[side]
        far[g, side] = (
            dv_send(g, dvs.at[g, row, x2, 0], 0, side, xp_dev),
            dv_send(g, dvs.at[g, row, x2, 1], 1, side, xm_dev),
        )
        close[g, side] = (
            dv_send(g, dvs.at[g, row, xp, 1], 2, side, xp_dev),
            dv_send(g, dvs.at[g, row, xm, 0], 3, side, xm_dev),
        )

    def dv_join(g, side):
        out = []
        for way in range(2):
            far[g, side][way].wait_recv()
            mine = dvs[g, sides[side], xp, 0] if way == 0 else dvs[g, sides[side], xm, 1]
            dvt[g, way, side] = (mine.astype(F32) + dvr[g, way, side].astype(F32)).astype(BF16)
            out.append(dv_send(g, dvt.at[g, way, side], 4 + way, side, xp_dev if way == 0 else xm_dev))
        joint[g, side] = out

    def chip_total(g, side, b):
        for copy in (close[g, side][1 - b], joint[g, side][b]):
            copy.wait_recv()
        one, two = (3, 4) if b == 0 else (2, 5)
        return (
            dvs[g, sides[side], x, b].astype(F32)
            + dvr[g, one, side].astype(F32)
            + dvr[g, two, side].astype(F32)
        )

    def dv_peer(g):
        to_y[g] = []
        for b in range(2):
            vgp[g, 0, b] = chip_total(g, 0, b).astype(BF16)
            to_y[g].append(send(vgp.at[g, 0, b], vgp.at[g, 1, b], dys.at[g, b], dyr.at[g, b], y4_dev))

    def dv_own(g):
        held_total[g] = [chip_total(g, 1, b) for b in range(2)]

    def dv_final(g):
        out = []
        for b in range(2):
            to_y[g][b].wait_recv()
            out.append((held_total[g][b] + vgp[g, 1, b].astype(F32)).astype(BF16))
        return out

    weigh(0)(0)
    weigh(1)(0)
    lay(0)
    dv_out(0, 0)
    gather_peer_forward(*keys_of[1])
    dv_join(0, 0)
    dv_out(0, 1)
    key_local[1].wait()
    key_core[1].wait_recv()
    gather_done(*keys_of[1])
    ring_step(4)
    weigh(0)(1)
    weigh(1)(1)
    lay(1)
    dv_out(1, 0)
    dv_peer(0)
    dv_join(0, 1)
    dv_join(1, 0)
    dv_out(1, 1)
    ring_step(5)
    dv_own(0)
    dv_peer(1)
    dv_join(1, 1)
    ring_step(6)

    def product_of(part, value_grad):
        for j in range(6):
            lanes = pl.ds(j * 384, 384)
            product = jnp.zeros((384, HD), F32)
            for b in range(2):
                product = product + lax.dot_general(
                    tok2[b, :, lanes], value_grad[b], (((0,), (0,)), ((), ())), preferred_element_type=F32
                )
            gb[part, pl.ds(j * 384, 384), :] = product

    ends = (pl.ds(0, 288), pl.ds(288, 288))

    def regroup(part):
        for j in range(NZ):
            for a in range(NYL):
                for h in range(2):
                    for k in range(NX):
                        to = (h * NYL + a) * 72 + j * 6
                        xb[part, k, pl.ds(to, 6), :] = gb[part, pl.ds(j * 192 + (a * 2 + h) * 24 + k * 6, 6), :]
        for k in range(NX):
            xbs[part, k] = xb[part, k].astype(BF16)

    def g_send(part, src, number, target):
        return send(src, xbr.at[part, number], bs.at[part, number], br.at[part, number], target)

    def g_far(part):
        return [
            g_send(part, xbs.at[part, x2, ends[0]], 0, xp_dev),
            g_send(part, xbs.at[part, x2, ends[1]], 1, xm_dev),
        ]

    def g_close(part):
        return [
            g_send(part, xbs.at[part, xp, ends[1]], 2, xp_dev),
            g_send(part, xbs.at[part, xm, ends[0]], 3, xm_dev),
        ]

    def g_join(part, copies):
        out = []
        for way, at, target in ((0, xp, xp_dev), (1, xm, xm_dev)):
            copies[way].wait_recv()
            xbt[part, way] = (xb[part, at, ends[way], :] + xbr[part, way].astype(F32)).astype(BF16)
            out.append(g_send(part, xbt.at[part, way], 4 + way, target))
        return out

    def g_total(part, close_pair, joint_pair):
        for end, one, two in ((0, 3, 4), (1, 2, 5)):
            close_pair[1 - end].wait_recv()
            joint_pair[end].wait_recv()
            yb[part, ends[end], :] = (
                xb[part, x, ends[end], :] + xbr[part, one].astype(F32) + xbr[part, two].astype(F32)
            )
        for k in range(NY):
            ybs[part, k] = yb[part, pl.ds(k * 72, 72), :].astype(BF16)
        out = []
        for d in (4, 3, 5, 2, 6, 1, 7):
            there = (y + d) % NY
            out.append(
                send(ybs.at[part, there], ybr.at[part, d], bys.at[part, d], byr.at[part, d], dev(z, there, x, c))
            )
        return out

    lt.wait()
    et.wait_recv()
    value_grad = dv_final(0)
    product_of(0, value_grad)
    regroup(0)
    far0 = g_far(0)
    close0 = g_close(0)
    dv_own(1)
    lw.wait()
    for i in range(NYL):
        ring_plus(6, i).wait_recv()
    weight = wbuf[...].reshape(48 * 48, 256)
    for b in range(2):
        vall[2 * chip + b] = jnp.dot(tok2[b], weight, preferred_element_type=F32).astype(BF16)
    gather_y(vall, vs, vr)
    joint0 = g_join(0, far0)
    value_grad = dv_final(1)
    product_of(1, value_grad)
    regroup(1)
    far1 = g_far(1)
    close1 = g_close(1)

    y0 = g_total(0, close0, joint0)
    joint1 = g_join(1, far1)
    gather_x(vall, vs, vr)
    y1 = g_total(1, close1, joint1)
    gather_peer(vall, vs, vr, 0)
    gather_peer(vall, vs, vr, 1)
    gather_x_forward(vall, vs, vr)
    gather_peer_forward(vall, vs, vr)
    for part, copies in ((0, y0), (1, y1)):
        for copy in copies:
            copy.wait_recv()
        total = yb[part, pl.ds(pl.multiple_of(y * 72, 8), 72), :]
        for d in range(1, NY):
            total = total + ybr[part, d].astype(F32)
        bsum[part] = total

    zs[...] = jnp.zeros((NZ, 2, 8, HD), F32)
    for j in range(NZ):
        for core in range(2):
            at = pl.ds(j * 6 + core * 3, 3)
            zs[j, core, 0:3, :] = bsum[0, at, :]
            zs[j, core, 3:6, :] = bsum[1, at, :]

    z_copies = []
    for d in (6, 5, 7, 4, 8, 3, 9, 2, 10, 1, 11, 0):
        there = (z + d) % NZ
        if d > 0:
            z_copies.append(
                send(zs.at[there, c], zr.at[0, d], zss.at[0, d], zrs.at[0, d], dev(there, y, x, c))
            )
        z_copies.append(
            send(zs.at[there, 1 - c], zr.at[1, d], zss.at[1, d], zrs.at[1, d], dev(there, y, x, 1 - c))
        )

    gather_done(vall, vs, vr)

    def attend(b):
        def group(g, carry):
            lanes = pl.ds(pl.multiple_of(g * HD, HD), HD)
            held = jnp.concatenate([vall[at, :, lanes] for at in key_at[b]], axis=0)
            for h in range(GROUP):
                head = pl.ds(pl.multiple_of((g * GROUP + h) * HD, HD), HD)
                flipped = lax.dot_general(
                    held, wts[b, g * GROUP + h], (((0,), (0,)), ((), ())), preferred_element_type=F32
                )
                att2[b, :, head] = flipped.T.astype(BF16)
            return carry

        lax.fori_loop(0, 2, group, 0)

    attend(0)
    attend(1)
    la = pltpu.make_async_copy(att2.at[c], att_out.at[:, wide], lsem.at[5])
    la.start()
    ea = send(att2.at[1 - c], att_out.at[:, wide], es.at[4], er.at[4], core_dev)
    for copy in z_copies:
        copy.wait_recv()
    mine, theirs = zs[z, c], zr[1, 0]
    for d in range(1, NZ):
        mine = mine + zr[0, d]
        theirs = theirs + zr[1, d]
    low, high = jnp.where(c == 0, mine, theirs), jnp.where(c == 0, theirs, mine)
    wg_out[:, 0:128] = low[0:3]
    wg_out[:, 128:256] = low[3:6]
    wg_out[:, 256:384] = high[0:3]
    wg_out[:, 384:512] = high[3:6]
    la.wait()
    ea.wait_recv()
    for copy in started:
        copy.wait_send()


def shards(tokens, queries, key_rows, out_grad, value_weight, documents, block_plan):
    anywhere = pl.BlockSpec(memory_space=pl.ANY)
    in_vmem = pl.BlockSpec(memory_space=pltpu.VMEM)
    dma = pltpu.SemaphoreType.DMA
    vmem = pltpu.VMEM
    attended, weight_grad = pl.pallas_call(
        body,
        out_shape=(
            jax.ShapeDtypeStruct((BLOCK, 2048), BF16),
            jax.ShapeDtypeStruct((3, 512), F32),
        ),
        in_specs=[anywhere] * 5 + [in_vmem, pl.BlockSpec(memory_space=pltpu.SMEM)],
        out_specs=(anywhere, in_vmem),
        scratch_shapes=[
            vmem((2, BLOCK, 2304), BF16),
            vmem((2, BLOCK, 1024), BF16),
            vmem((2, BLOCK, 1024), BF16),
            vmem((16, BLOCK, HD), BF16),
            vmem((16, BLOCK, HD), BF16),
            vmem((16, BLOCK, 256), BF16),
            vmem((48, 48, 256), BF16),
            vmem((2, 5 * BLOCK, BLOCK), F32),
            vmem((2, 8, 5 * BLOCK, BLOCK), BF16),
            vmem((2, 6, BLOCK, 256), F32),
            vmem((2, 2, NX, 2, BLOCK, HD), BF16),
            vmem((2, 6, 2, BLOCK, HD), BF16),
            vmem((2, 2, 2, BLOCK, HD), BF16),
            vmem((2, 2, 2, BLOCK, HD), BF16),
            vmem((2, BLOCK, 1024), BF16),
            vmem((2, 2304, HD), F32),
            vmem((2, NX, 576, HD), F32),
            vmem((2, NX, 576, HD), BF16),
            vmem((2, 6, 288, HD), BF16),
            vmem((2, 2, 288, HD), BF16),
            vmem((2, 576, HD), F32),
            vmem((2, NY, 72, HD), BF16),
            vmem((2, NY, 72, HD), BF16),
            vmem((2, 72, HD), F32),
            vmem((NZ, 2, 8, HD), F32),
            vmem((2, NZ, 8, HD), F32),
            dma((8,)),
            dma((7,)), dma((7,)),
            dma((4,)), dma((4,)),
            dma((2, 6, 4)), dma((2, 6, 4)),
            dma((2, 7, 2)), dma((2, 7, 2)),
            dma((7, 2)), dma((7, 2)),
            dma((2, 6, 2)), dma((2, 6, 2)),
            dma((2, 2)), dma((2, 2)),
            dma((2, 6)), dma((2, 6)),
            dma((2, NY)), dma((2, NY)),
            dma((2, NZ)), dma((2, NZ)),
        ],
        compiler_params=pltpu.CompilerParams(
            collective_id=0, has_side_effects=True, vmem_limit_bytes=60 * 1024 * 1024
        ),
        name="value_path",
    )(
        tokens[0], queries[0], key_rows[0], out_grad[0], value_weight,
        documents.reshape(16, BLOCK), block_plan,
    )
    return attended[None], weight_grad


def solution(mesh):
    in_specs = (
        P("fsdp", "seq", None),
        P("fsdp", "seq", None),
        P("fsdp", "seq", None),
        P("fsdp", "seq", None),
        P("fsdp", None),
        P("fsdp", None),
        P("fsdp", None),
    )
    out_specs = (P("fsdp", "seq", None), P(("fsdp", "seq"), None))
    return jax.shard_map(shards, mesh=mesh, in_specs=in_specs, out_specs=out_specs, check_vma=False)
```

time: 93.1 us -> 86.9 us (0.933)
  Pallas kernels: 89.8 us -> 83.5 us
    pallas_call x1, Pallas kernels: 89.8 us -> 83.5 us  [shards(): pl.pallas_call(body, out_shape=(jax.ShapeDtypeStruct((BLOCK, 2048), BF16)...]
where the time goes in v3:
time: 86.9 us; the launch traced here: 86.7 us
  Pallas kernels  83.5 us (96%)
  local copies, waits for them, and re-layouts  2.49 us (3%)
    pallas_call x1, Pallas kernels, shards(): pl.pallas_call(body, out_shape=(jax.ShapeDtypeStruct((BLOCK, 2048), BF16)...  83.5 us
    unnamed x4, local copies, waits for them, and re-layouts  2.49 us

profile of v3, /device:TPU:1, one launch (start us, length us, event | category | flops | bytes accessed | tf_op | source)
XLA Modules:
  0.0 86.7 jit_solution(3986650841342632255)
XLA Ops:
  0.6 83.5 %value_path.1 = (bf16[128,2048]{1,0:T(8,128)(2,1)}, f32[3,512]{1,0:T(4,128)}) custom-call(bf16[128,2304]{1,0:T(8,128)(2,1)} %bitcast.6, bf16[128,2048]{1,0:T(8,128)(2,1)} %bitcast.8, bf16[128,512]{1,0:T(8,128)(2,1)} %bitcast.10, bf16[128,2048]{1,0:T(8,128)(2,1)} %bitcast.9, bf16[48,512]{1,0:T(8,128)(2,1)} %w_hbm.1, s32[16,128]{1,0:T(8,128)} %bitcast.11, ...), custom_call_target="tpu_custom_call" | custom-call | tf_op jit(solution)/shard_map/value_path/pallas_call | solution.py:494
  84.2 0.0 copy-start
  84.2 1.9 %copy.11 = bf16[1,128,2048]{2,1,0:T(8,128)(2,1)} copy(bf16[1,128,2048]{2,1,0:T(8,128)(2,1)} %bitcast.7) | data formatting | bytes 1048576
  86.1 0.0 copy-done
  86.1 0.6 copy.12
Async XLA Ops:
  84.2 1.9 %copy-start = (f32[3,512]{1,0:T(4,128)S(1)}, f32[3,512]{1,0:T(4,128)}, u32[]{:S(2)}) copy-start(f32[3,512]{1,0:T(4,128)} %get-tuple-element.9) | copy-start | bytes 18436

commit v4 on v3

--- a/solution.py
+++ b/solution.py
@@ -126,10 +126,11 @@
     def gather_x_forward(buf, ss, rs):
         pass_on(buf, ss, rs, yh, (1, 2), 5)
 
-    def gather_peer(buf, ss, rs, block):
-        arrived(buf, ss, rs, 0, block).wait_recv()
-        peer = buf.at[unit(1 - yh, x, block)]
-        for kind, target in ((3, xp_dev), (4, xm_dev)) if block == 0 else ((4, xm_dev), (3, xp_dev)):
+    def gather_peer(buf, ss, rs):
+        for block in range(2):
+            arrived(buf, ss, rs, 0, block).wait_recv()
+        for block, kind, target in ((0, 3, xp_dev), (1, 4, xm_dev), (1, 3, xp_dev), (0, 4, xm_dev)):
+            peer = buf.at[unit(1 - yh, x, block)]
             send(peer, peer, ss.at[kind, block], rs.at[kind, block], target)
 
     def gather_peer_forward(buf, ss, rs):
@@ -199,12 +200,10 @@
     lt.start()
 
     gather_x_forward(*keys_of[1])
-    gather_peer(*keys_of[0], 0)
-    gather_peer(*keys_of[0], 1)
+    gather_peer(*keys_of[0])
     ring_step(2)
     gather_peer_forward(*keys_of[0])
-    gather_peer(*keys_of[1], 0)
-    gather_peer(*keys_of[1], 1)
+    gather_peer(*keys_of[1])
     lq.wait()
     eq.wait_recv()
     ld.wait()
@@ -418,8 +417,7 @@
     joint1 = g_join(1, far1)
     gather_x(vall, vs, vr)
     y1 = g_total(1, close1, joint1)
-    gather_peer(vall, vs, vr, 0)
-    gather_peer(vall, vs, vr, 1)
+    gather_peer(vall, vs, vr)
     gather_x_forward(vall, vs, vr)
     gather_peer_forward(vall, vs, vr)
     for part, copies in ((0, y0), (1, y1)):
@@ -450,25 +448,26 @@
 
     gather_done(vall, vs, vr)
 
-    def attend(b):
-        def group(g, carry):
-            lanes = pl.ds(pl.multiple_of(g * HD, HD), HD)
-            held = jnp.concatenate([vall[at, :, lanes] for at in key_at[b]], axis=0)
-            for h in range(GROUP):
-                head = pl.ds(pl.multiple_of((g * GROUP + h) * HD, HD), HD)
-                flipped = lax.dot_general(
-                    held, wts[b, g * GROUP + h], (((0,), (0,)), ((), ())), preferred_element_type=F32
-                )
-                att2[b, :, head] = flipped.T.astype(BF16)
-            return carry
-
-        lax.fori_loop(0, 2, group, 0)
-
-    attend(0)
-    attend(1)
-    la = pltpu.make_async_copy(att2.at[c], att_out.at[:, wide], lsem.at[5])
-    la.start()
-    ea = send(att2.at[1 - c], att_out.at[:, wide], es.at[4], er.at[4], core_dev)
+    def attend(b, g):
+        held = jnp.concatenate([vall[at, :, pl.ds(g * HD, HD)] for at in key_at[b]], axis=0)
+        for h in range(g * GROUP, g * GROUP + GROUP):
+            flipped = lax.dot_general(
+                held, wts[b, h], (((0,), (0,)), ((), ())), preferred_element_type=F32
+            )
+            att2[b, :, pl.ds(h * HD, HD)] = flipped.T.astype(BF16)
+
+    att_local, att_core = [], []
+    for g in range(2):
+        attend(0, g)
+        attend(1, g)
+        part = pl.ds(g * 512, 512)
+        there = pl.ds(pl.multiple_of(c * 1024 + g * 512, 512), 512)
+        att_core.append(
+            send(att2.at[1 - c, :, part], att_out.at[:, there], es.at[(4, 7)[g]], er.at[(4, 7)[g]], core_dev)
+        )
+        copy = pltpu.make_async_copy(att2.at[c, :, part], att_out.at[:, there], lsem.at[(5, 8)[g]])
+        copy.start()
+        att_local.append(copy)
     for copy in z_copies:
         copy.wait_recv()
     mine, theirs = zs[z, c], zr[1, 0]
@@ -480,8 +479,10 @@
     wg_out[:, 128:256] = low[3:6]
     wg_out[:, 256:384] = high[0:3]
     wg_out[:, 384:512] = high[3:6]
-    la.wait()
-    ea.wait_recv()
+    for copy in att_local:
+        copy.wait()
+    for copy in att_core:
+        copy.wait_recv()
     for copy in started:
         copy.wait_send()
 
@@ -526,8 +527,8 @@
             vmem((2, 72, HD), F32),
             vmem((NZ, 2, 8, HD), F32),
             vmem((2, NZ, 8, HD), F32),
-            dma((8,)),
-            dma((7,)), dma((7,)),
+            dma((9,)),
+            dma((8,)), dma((8,)),
             dma((4,)), dma((4,)),
             dma((2, 6, 4)), dma((2, 6, 4)),
             dma((2, 7, 2)), dma((2, 7, 2)),

time: 86.9 us -> 85.4 us (0.983)
  Pallas kernels: 83.5 us -> 82 us
    pallas_call x1, Pallas kernels: 83.5 us -> 82 us  [shards(): pl.pallas_call(body, out_shape=(jax.ShapeDtypeStruct((BLOCK, 2048), BF16)...]
where the time goes in v4:
time: 85.4 us; the launch traced here: 85.2 us
  Pallas kernels  82 us (96%)
  local copies, waits for them, and re-layouts  2.49 us (3%)
    pallas_call x1, Pallas kernels, shards(): pl.pallas_call(body, out_shape=(jax.ShapeDtypeStruct((BLOCK, 2048), BF16)...  82 us
    unnamed x4, local copies, waits for them, and re-layouts  2.49 us

profile of v4, /device:TPU:1, one launch (start us, length us, event | category | flops | bytes accessed | tf_op | source)
XLA Modules:
  0.0 85.2 jit_solution(7207192054220764635)
XLA Ops:
  0.6 82.0 %value_path.1 = (bf16[128,2048]{1,0:T(8,128)(2,1)}, f32[3,512]{1,0:T(4,128)}) custom-call(bf16[128,2304]{1,0:T(8,128)(2,1)} %bitcast.6, bf16[128,2048]{1,0:T(8,128)(2,1)} %bitcast.8, bf16[128,512]{1,0:T(8,128)(2,1)} %bitcast.10, bf16[128,2048]{1,0:T(8,128)(2,1)} %bitcast.9, bf16[48,512]{1,0:T(8,128)(2,1)} %w_hbm.1, s32[16,128]{1,0:T(8,128)} %bitcast.11, ...), custom_call_target="tpu_custom_call" | custom-call | tf_op jit(solution)/shard_map/value_path/pallas_call | solution.py:495
  82.7 0.0 copy-start
  82.7 1.9 %copy.11 = bf16[1,128,2048]{2,1,0:T(8,128)(2,1)} copy(bf16[1,128,2048]{2,1,0:T(8,128)(2,1)} %bitcast.7) | data formatting | bytes 1048576
  84.6 0.0 copy-done
  84.6 0.6 copy.12
Async XLA Ops:
  82.7 1.9 %copy-start = (f32[3,512]{1,0:T(4,128)S(1)}, f32[3,512]{1,0:T(4,128)}, u32[]{:S(2)}) copy-start(f32[3,512]{1,0:T(4,128)} %get-tuple-element.9) | copy-start | bytes 18436
